TPU v7x, 32 devices: a whole 2x2x4 slice. The times are simulated.
32 devices in a mesh: row: 4 (over y, x), col: 8 (over z, core).
Axes of the slice: x: 2, y: 2, z: 4, core: 2. Of those that a mesh axis runs over, the one named last changes fastest.
Arguments:
- image: bfloat16 [64, 256, 768], P('row', 'col'), may hold values from -6 to 6
- conv_taps: float32 [9, 768], replicated, may hold values from -0.5 to 0.5
- w_query: bfloat16 [768, 768], replicated, may hold values from -0.21875 to 0.21875
- w_key: bfloat16 [768, 768], replicated, may hold values from -0.21875 to 0.21875
- w_value: bfloat16 [768, 768], replicated, may hold values from -0.21875 to 0.21875
- w_out: bfloat16 [768, 768], replicated, may hold values from -0.21875 to 0.21875
- grad_out: bfloat16 [64, 256, 768], P('row', 'col'), may hold values from -6 to 6
Outputs:
- grad_image: bfloat16 [64, 256, 768], P('row', 'col')
- grad_weights: float32 [768, 3072], P(None, 'col')
- grad_conv: float32 [9, 768], P(None, 'col')
All inputs are finite; a program needn't handle non-finite values.
Results may differ from a plain program's by a relative error of at most 0.022.
Values may be sent and summed in bfloat16 or wider, within the bound.
A program may use at most 128 MiB of HBM per device.

v0:
```python
from functools import partial
import math

import jax
import jax.numpy as jnp
from jax import lax
from jax.sharding import PartitionSpec as P

HEADS = 12
HD = 64
POOL = 8


EPSILON = 1e-05


def with_halo(cells, sides, width):
    for axis, dim in sides:
        count = lax.axis_size(axis)
        ends = count - 1
        head = lax.slice_in_dim(cells, 0, width, axis=dim)
        tail = lax.slice_in_dim(cells, cells.shape[dim] - width, cells.shape[dim], axis=dim)
        cells = jnp.concatenate(
            [
                lax.ppermute(tail, axis, [(i, (i + 1) % count) for i in range(ends)]),
                cells,
                lax.ppermute(head, axis, [((i + 1) % count, i) for i in range(ends)]),
            ],
            axis=dim,
        )
    return cells


def contract_first(left, right):
    return lax.dot_general(
        left, right, (((0,), (0,)), ((), ())), preferred_element_type=jnp.float32
    )


def contract_last(left, right):
    return lax.dot_general(
        left, right, (((1,), (1,)), ((), ())), preferred_element_type=jnp.float32
    )


def exact_first(left, right):
    return lax.dot_general(
        left,
        right,
        (((0,), (0,)), ((), ())),
        precision=lax.Precision.HIGHEST,
        preferred_element_type=jnp.float32,
    )


def exact_last(left, right):
    return lax.dot_general(
        left,
        right,
        (((1,), (1,)), ((), ())),
        precision=lax.Precision.HIGHEST,
        preferred_element_type=jnp.float32,
    )


def stencil(padded, taps, height, width, flipped):
    total = jnp.zeros((height, width, padded.shape[2]), jnp.float32)
    for tap_row in range(3):
        for tap_col in range(3):
            if flipped:
                window = padded[
                    2 - tap_row : 2 - tap_row + height, 2 - tap_col : 2 - tap_col + width
                ]
            else:
                window = padded[tap_row : tap_row + height, tap_col : tap_col + width]
            total = total + taps[3 * tap_row + tap_col] * window.astype(jnp.float32)
    return total


def attend(carry, inputs, key_heads, value_heads):
    grad_key, grad_value = carry
    query_block, dout_block = inputs
    softmax_scale = HD ** (-0.5)
    query_heads = query_block.reshape(-1, HEADS, HD)
    dout_heads = dout_block.reshape(-1, HEADS, HD)
    scores = (
        jnp.einsum("qhd,khd->hqk", query_heads, key_heads, preferred_element_type=jnp.float32)
        * softmax_scale
    )
    expons = jnp.exp(scores)
    probabilities = expons / jnp.sum(expons, axis=-1, keepdims=True)
    weights = probabilities.astype(jnp.bfloat16)
    attended = jnp.einsum(
        "hqk,khd->qhd", weights, value_heads, preferred_element_type=jnp.float32
    ).astype(jnp.bfloat16)
    grad_probs = jnp.einsum(
        "qhd,khd->hqk", dout_heads, value_heads, preferred_element_type=jnp.float32
    )
    deltas = jnp.einsum("qhd,qhd->hq", dout_heads, attended, preferred_element_type=jnp.float32)
    grad_scores = (probabilities * (grad_probs - deltas[:, :, None]) * softmax_scale).astype(
        jnp.bfloat16
    )
    grad_query = jnp.einsum(
        "hqk,khd->qhd", grad_scores, key_heads, preferred_element_type=jnp.float32
    ).astype(jnp.bfloat16)
    grad_key = grad_key + jnp.einsum(
        "hqk,qhd->khd", grad_scores, query_heads, preferred_element_type=jnp.float32
    )
    grad_value = grad_value + jnp.einsum(
        "hqk,qhd->khd", weights, dout_heads, preferred_element_type=jnp.float32
    )
    return (
        (grad_key, grad_value),
        (attended.reshape(query_block.shape), grad_query.reshape(query_block.shape)),
    )


def on_device(image, conv_taps, w_query, w_key, w_value, w_out, grad_out):
    height, width, channels = image.shape
    padded = with_halo(image, (("row", 0), ("col", 1)), 1)
    mixed = image.astype(jnp.float32) + stencil(padded, conv_taps, height, width, False)
    hidden = mixed.astype(jnp.bfloat16)
    flat_hidden = hidden.reshape(-1, channels)
    query = jnp.dot(flat_hidden, w_query, preferred_element_type=jnp.float32).astype(jnp.bfloat16)
    pooled = (
        hidden.astype(jnp.float32)
        .reshape(height // POOL, POOL, width // POOL, POOL, channels)
        .mean(axis=(1, 3))
    )
    centre = jnp.mean(pooled, axis=-1, keepdims=True)
    spread = jnp.mean(jnp.square(pooled - centre), axis=-1, keepdims=True)
    inverse = lax.rsqrt(spread + EPSILON)
    standard = (pooled - centre) * inverse
    normed = standard.astype(jnp.bfloat16)
    gathered = lax.all_gather(normed, "col", axis=1, tiled=True)
    pooled_rows, pooled_cols = (gathered.shape[0], gathered.shape[1])
    key_cells = gathered.reshape(-1, channels)
    keys = jnp.dot(key_cells, w_key, preferred_element_type=jnp.float32).astype(jnp.bfloat16)
    values = jnp.dot(key_cells, w_value, preferred_element_type=jnp.float32).astype(jnp.bfloat16)
    flat_grad = grad_out.reshape(-1, channels)
    dout = contract_last(flat_grad, w_out).astype(jnp.bfloat16)
    total_rows = flat_hidden.shape[0]
    block_rows = math.gcd(total_rows, 512)
    blocks = total_rows // block_rows
    key_heads = keys.reshape(-1, HEADS, HD)
    value_heads = values.reshape(-1, HEADS, HD)
    empty_grad = jnp.zeros(key_heads.shape, jnp.float32)
    carry, produced = lax.scan(
        partial(attend, key_heads=key_heads, value_heads=value_heads),
        (empty_grad, empty_grad),
        (query.reshape(blocks, block_rows, channels), dout.reshape(blocks, block_rows, channels)),
    )
    grad_key = carry[0].reshape(pooled_rows, pooled_cols, channels)
    grad_value = carry[1].reshape(pooled_rows, pooled_cols, channels)
    attended = produced[0].reshape(-1, channels)
    grad_query = produced[1].reshape(-1, channels)
    grad_wout = contract_first(attended, flat_grad)
    grad_wquery = contract_first(flat_hidden, grad_query)
    grad_hidden = contract_last(grad_query, w_query)
    key_float = w_key.astype(jnp.float32)
    value_float = w_value.astype(jnp.float32)
    flat_key = grad_key.reshape(-1, channels)
    flat_value = grad_value.reshape(-1, channels)
    cell_terms = exact_last(flat_key, key_float) + exact_last(flat_value, value_float)
    cells_float = key_cells.astype(jnp.float32)
    grad_wkey = exact_first(cells_float, flat_key)
    grad_wvalue = exact_first(cells_float, flat_value)
    grad_normed = lax.psum_scatter(
        cell_terms.reshape(pooled_rows, pooled_cols, channels).astype(jnp.bfloat16),
        "col",
        scatter_dimension=1,
        tiled=True,
    ).astype(jnp.float32)
    grad_pooled = (
        grad_normed
        - jnp.mean(grad_normed, axis=-1, keepdims=True)
        - standard * jnp.mean(grad_normed * standard, axis=-1, keepdims=True)
    ) * inverse
    spread_back = jnp.broadcast_to(
        (grad_pooled / (POOL * POOL))[:, None, :, None, :],
        (height // POOL, POOL, width // POOL, POOL, channels),
    ).reshape(height, width, channels)
    grad_mixed = (
        grad_out.astype(jnp.float32) + grad_hidden.reshape(height, width, channels) + spread_back
    )
    grad_padded = with_halo(grad_mixed.astype(jnp.bfloat16), (("row", 0), ("col", 1)), 1).astype(
        grad_mixed.dtype
    )
    grad_image = (grad_mixed + stencil(grad_padded, conv_taps, height, width, True)).astype(
        jnp.bfloat16
    )
    tap_list = []
    for tap_row in range(3):
        for tap_col in range(3):
            window = padded[tap_row : tap_row + height, tap_col : tap_col + width].astype(
                jnp.float32
            )
            tap_list.append(jnp.sum(grad_mixed * window, axis=(0, 1)))
    tap_terms = jnp.stack(tap_list, axis=0)
    weight_terms = jnp.concatenate([grad_wquery, grad_wkey, grad_wvalue, grad_wout], axis=1)
    column_sums = (
        lax.psum_scatter(
            weight_terms.astype(jnp.bfloat16), "col", scatter_dimension=1, tiled=True
        ).astype(jnp.float32),
        lax.psum_scatter(
            tap_terms.astype(jnp.bfloat16), "col", scatter_dimension=1, tiled=True
        ).astype(jnp.float32),
    )
    grad_weights, grad_conv = (
        lax.psum(column_sums[0].astype(jnp.bfloat16), "row").astype(jnp.float32),
        lax.psum(column_sums[1].astype(jnp.bfloat16), "row").astype(jnp.float32),
    )
    return (grad_image, grad_weights, grad_conv)


def solution(mesh):
    return jax.shard_map(
        on_device,
        mesh=mesh,
        in_specs=(P("row", "col", None), P(), P(), P(), P(), P(), P("row", "col", None)),
        out_specs=(P("row", "col", None), P(None, "col"), P(None, "col")),
        check_vma=False,
    )
```

profile of v0, /device:TPU:0, one launch (start us, length us, event | category | flops | bytes accessed | tf_op | source)
XLA Modules:
  0.0 293.8 jit_solution(12890035376737956254)
XLA Ops:
  8.1 4.9 %collective-permute-start = (bf16[1,32,768]{2,1,0:T(8,128)(2,1)S(1)}, bf16[1,32,768]{2,1,0:T(8,128)(2,1)S(1)}, u32[]{:S(2)}, u32[]{:S(2)}) collective-permute-start(bf16[1,32,768]{2,1,0:T(8,128)(2,1)S(1)} %get-tuple-element.78), channel_id=1, source_target_pairs={{0,8},{8,16},{16,24},{1,9},{9,17},{17,25},{2,10},{10,18},{18,26},{... | collective-permute-start | bytes 147464 | tf_op jit(solution)/shard_map/ppermute | solution.py:25
  14.3 2.4 convolution_convert_fusion.4
  16.8 2.2 collective-permute-done.1
  21.2 3.7 %collective-permute-start.2 = (bf16[18,1,768]{2,1,0:T(2,128)(2,1)}, bf16[18,1,768]{2,1,0:T(2,128)(2,1)}, u32[]{:S(2)}, u32[]{:S(2)}) collective-permute-start(bf16[18,1,768]{2,1,0:T(2,128)(2,1)} %get-tuple-element.75), channel_id=1, source_target_pairs={{0,1},{1,2},{2,3},{3,4},{4,5},{5,6},{6,7},{8,9},{9,10},{10,11},{11... | collective-permute-start | bytes 82952 | tf_op jit(solution)/shard_map/ppermute | solution.py:25
  27.7 5.4 %fusion.28 = bf16[16,32,768]{2,1,0:T(8,128)(2,1)S(1)} fusion(bf16[16,32,768]{2,1,0:T(8,128)(2,1)S(1)} %copy-done.5, bf16[1,32,768]{2,1,0:T(8,128)(2,1)} %copy-done.23, bf16[1,32,768]{2,1,0:T(8,128)(2,1)} %copy-done.22, f32[768]{0:T(1024)} %get-tuple-element.69, f32[768]{0:T(1024)} %get-tuple-element.70, f32[768]{0:T(1024)S(1)} %get-tuple-element.63, ...), kind=kLoop, calls=%fused_computation.62 | loop fusion | flops 20447232 | bytes 2638848 | tf_op jit(solution)/shard_map/convert_element_type | solution.py:122
  34.1 1.7 convolution_convert_fusion.5
  35.7 2.4 copy.51
  40.3 14.0 %all_gather.3 = bf16[2,32,768]{2,0,1:T(2,128)(2,1)S(1)} all-gather(bf16[2,4,768]{2,0,1:T(2,128)(2,1)S(1)} %copy.49), channel_id=1, replica_groups=mesh['row'=4,'col'=8] {'col'}, dimensions={1}, use_global_device_ids=true | all-gather | bytes 110592 | tf_op jit(solution)/shard_map/all_gather | solution.py:135
  57.9 1.8 fusion.42
  59.7 2.6 fusion.63
  64.6 3.3 %fusion.32 = f32[12,64,64]{2,1,0:T(8,128)} fusion(bf16[512,12,64]{0,2,1:T(8,128)(2,1)} %bitcast.91, f32[12,512,64]{1,2,0:T(8,128)S(1)} %fusion.42, f32[12,512,64]{1,2,0:T(8,128)} %fusion.63, bf16[12,512,64]{1,2,0:T(8,128)(2,1)S(1)} %bitcast.81, bf16[12,64,512]{2,1,0:T(8,128)(2,1)} %convolution_convert_fusion.7), kind=kOutput, calls=%fused_computation.86 | convolution fusion | flops 53090368 | bytes 5701632 | tf_op jit(solution)/shard_map/while/body/eval_jaxpr/hqk,qhd->khd/dot_general | solution.py:106
  67.9 3.3 %convolution_convert_fusion.6 = bf16[12,64,512]{2,1,0:T(8,128)(2,1)} fusion(bf16[64,12,64]{0,2,1:T(8,128)(2,1)} %bitcast.103, f32[12,512,64]{1,2,0:T(8,128)S(1)} %fusion.42, f32[12,512,64]{1,2,0:T(8,128)} %fusion.63, bf16[12,512,64]{1,2,0:T(8,128)(2,1)S(1)} %bitcast.82, bf16[12,64,512]{2,1,0:T(8,128)(2,1)} %convolution_convert_fusion.7), kind=kOutput, calls=%fused_computation.74 | convolution fusion | flops 53483584 | bytes 5603328 | tf_op jit(solution)/shard_map/while/body/eval_jaxpr/hqk,khd->qhd/dot_general | solution.py:103
  71.2 2.8 fusion.62
  74.0 2.1 convolution_convert_fusion.2
  76.1 1.9 fusion.31
  78.3 1.8 convolution_convert_fusion.1
  80.2 1.8 convolution_convert_fusion
  82.0 2.1 convolution_convert_fusion.3
  84.1 2.9 copy.57
  87.1 2.0 dot_general.72
  89.1 42.7 %all-reduce.6.cloned.1.call-done = bf16[2,32,768]{2,1,0:T(8,128)(2,1)} async-done(((bf16[2,32,768]{2,1,0:T(8,128)(2,1)}), bf16[2,32,768]{2,1,0:T(8,128)(2,1)}) %all-reduce.6.cloned.1.call-update) | async-done | bytes 98320
  133.8 6.3 %fusion.16 = (bf16[768]{0:T(1024)(128)(2,1)S(1)}, bf16[768]{0:T(1024)(128)(2,1)S(1)}, bf16[768]{0:T(1024)(128)(2,1)S(1)}, bf16[768]{0:T(1024)(128)(2,1)S(1)}, bf...) fusion(bf16[18,1,768]{2,1,0:T(2,128)(2,1)} %collective-permute-, ...), kind=kOutput, calls=%fused_computation.36 | convolution fusion | flops 625599744 | bytes 8523264 | tf_op jit(solution)/shard_map/dot_general | solution.py:41
  145.4 2.6 stack.49
  149.7 4.3 %pad_maximum_fusion = bf16[768,3072]{0,1:T(8,128)(2,1)} fusion(bf16[768,768]{0,1:T(8,128)(2,1)} %convolution_convert_fusion.1, bf16[768,768]{0,1:T(8,128)(2,1)S(1)} %copy-done.1, bf16[768,768]{0,1:T(8,128)(2,1)S(1)} %copy-done.2, bf16[768,768]{0,1:T(8,128)(2,1)} %convolution_convert_fusion), kind=kLoop, calls=%fused_computation.1 | loop fusion | flops 18874368 | bytes 9437184 | tf_op jit(solution)/shard_map/concatenate | solution.py:200
  156.5 4.5 %collective-permute-start.4 = (bf16[1,32,768]{2,1,0:T(8,128)(2,1)S(1)}, bf16[1,32,768]{2,1,0:T(8,128)(2,1)S(1)}, u32[]{:S(2)}, u32[]{:S(2)}) collective-permute-start(bf16[1,32,768]{2,1,0:T(8,128)(2,1)S(1)} %get-tuple-element.76), channel_id=1, source_target_pairs={{0,8},{8,16},{16,24},{1,9},{9,17},{17,25},{2,10},{10,18},{18,26},{... | collective-permute-start | bytes 147464 | tf_op jit(solution)/shard_map/ppermute | solution.py:25
  164.2 3.0 %collective-permute-start.6 = (bf16[18,1,768]{2,1,0:T(2,128)(2,1)S(1)}, bf16[18,1,768]{2,1,0:T(2,128)(2,1)S(1)}, u32[]{:S(2)}, u32[]{:S(2)}) collective-permute-start(bf16[18,1,768]{2,1,0:T(2,128)(2,1)S(1)} %get-tuple-element.72), channel_id=1, source_target_pairs={{0,1},{1,2},{2,3},{3,4},{4,5},{5,6},{6,7},{8,9},{9,10},{10,11},{11... | collective-permute-start | bytes 82952 | tf_op jit(solution)/shard_map/ppermute | solution.py:25
  167.2 15.0 %reduce-scatter.8.cloned.1.call-done = bf16[96,9]{1,0:T(8,128)(2,1)} async-done(((bf16[768,9]{1,0:T(8,128)(2,1)}), bf16[96,9]{1,0:T(8,128)(2,1)}) %reduce-scatter.8.cloned.1.call-update) | async-done | bytes 1744
  183.0 9.8 %psum.15 = bf16[9,96]{1,0:T(8,128)(2,1)S(1)} all-reduce(bf16[9,96]{1,0:T(8,128)(2,1)S(1)} %copy.70), channel_id=1, replica_groups=mesh['row'=4,'col'=8] {'row'}, use_global_device_ids=true, to_apply=%region_19.20 | all-reduce | flops 864 | bytes 3456 | tf_op jit(solution)/shard_map/psum | solution.py:211
  193.4 44.2 %reduce-scatter.6.cloned.1.call-done = bf16[768,384]{0,1:T(8,128)(2,1)} async-done(((bf16[768,3072]{0,1:T(8,128)(2,1)}), bf16[768,384]{0,1:T(8,128)(2,1)}) %reduce-scatter.6.cloned.1.call-update) | async-done | bytes 589840 | tf_op jit(solution)/shard_map/reduce_scatter | solution.py:202
  239.1 2.6 fusion.20
  241.6 43.3 %all-reduce.4.cloned.1.call-done = bf16[768,384]{0,1:T(8,128)(2,1)} async-done(((bf16[768,384]{0,1:T(8,128)(2,1)}), bf16[768,384]{0,1:T(8,128)(2,1)}) %all-reduce.4.cloned.1.call-update) | async-done | bytes 589840 | tf_op jit(solution)/shard_map/psum | solution.py:210
  285.0 2.3 copy.58
  (130 shorter events, 33.1 us)
Async XLA Ops:
  7.2 26.9 %copy-start = (bf16[768,768]{1,0:T(8,128)(2,1)S(1)}, bf16[768,768]{1,0:T(8,128)(2,1)}, u32[]{:S(2)}) copy-start(bf16[768,768]{1,0:T(8,128)(2,1)} %param.9) | copy-start | bytes 3538948
  7.2 124.6 %all-reduce.6.cloned.1.call-start = ((), (), s32[]{:S(2)}) async-start(), calls=%async_computation.5 | async-start | bytes 196608
  8.1 8.6 %collective-permute-start = (bf16[1,32,768]{2,1,0:T(8,128)(2,1)S(1)}, bf16[1,32,768]{2,1,0:T(8,128)(2,1)S(1)}, u32[]{:S(2)}, u32[]{:S(2)}) collective-permute-start(bf16[1,32,768]{2,1,0:T(8,128)(2,1)S(1)} %get-tuple-element.78), channel_id=1, source_target_pairs={{0,8},{8,16},{16,24},{1,9},{9,17},{17,25},{2,10},{10,18},{18,26},{... | collective-permute-start | bytes 147464 | tf_op jit(solution)/shard_map/ppermute | solution.py:25
  13.0 6.0 %collective-permute-start.1 = (bf16[1,32,768]{2,1,0:T(8,128)(2,1)S(1)}, bf16[1,32,768]{2,1,0:T(8,128)(2,1)S(1)}, u32[]{:S(2)}, u32[]{:S(2)}) collective-permute-start(bf16[1,32,768]{2,1,0:T(8,128)(2,1)S(1)} %get-tuple-element.79), channel_id=1, source_target_pairs={{8,0},{16,8},{24,16},{9,1},{17,9},{25,17},{10,2},{18,10},{26,18},{... | collective-permute-start | bytes 147464 | tf_op jit(solution)/shard_map/ppermute | solution.py:27
  14.3 2.5 copy-start.5
  16.7 8.1 %copy-start.33 = (f32[9,768]{1,0:T(8,128)S(1)}, f32[9,768]{1,0:T(8,128)}, u32[]{:S(2)}) copy-start(f32[9,768]{1,0:T(8,128)} %param.8) | copy-start | bytes 82948
  16.7 8.8 %copy-start.22 = (bf16[1,32,768]{2,1,0:T(8,128)(2,1)}, bf16[1,32,768]{2,1,0:T(8,128)(2,1)S(1)}, u32[]{:S(2)}) copy-start(bf16[1,32,768]{2,1,0:T(8,128)(2,1)S(1)} %collective-permute-done) | copy-start | bytes 147460
  19.0 6.5 %copy-start.23 = (bf16[1,32,768]{2,1,0:T(8,128)(2,1)}, bf16[1,32,768]{2,1,0:T(8,128)(2,1)S(1)}, u32[]{:S(2)}) copy-start(bf16[1,32,768]{2,1,0:T(8,128)(2,1)S(1)} %collective-permute-done.1) | copy-start | bytes 147460
  19.0 6.5 %copy-start.17 = (bf16[18,32,768]{2,1,0:T(8,128)(2,1)}, bf16[18,32,768]{2,1,0:T(8,128)(2,1)S(1)}, u32[]{:S(2)}) copy-start(bf16[18,32,768]{2,1,0:T(8,128)(2,1)S(1)} %constant_dynamic-update-slice_fusion) | copy-start | bytes 2654212
  19.9 7.8 %collective-permute-start.3 = (bf16[18,1,768]{2,1,0:T(2,128)(2,1)}, bf16[18,1,768]{2,1,0:T(2,128)(2,1)}, u32[]{:S(2)}, u32[]{:S(2)}) collective-permute-start(bf16[18,1,768]{2,1,0:T(2,128)(2,1)} %get-tuple-element.74), channel_id=1, source_target_pairs={{1,0},{2,1},{3,2},{4,3},{5,4},{6,5},{7,6},{9,8},{10,9},{11,10},{12... | collective-permute-start | bytes 82952 | tf_op jit(solution)/shard_map/ppermute | solution.py:27
  21.2 6.5 %collective-permute-start.2 = (bf16[18,1,768]{2,1,0:T(2,128)(2,1)}, bf16[18,1,768]{2,1,0:T(2,128)(2,1)}, u32[]{:S(2)}, u32[]{:S(2)}) collective-permute-start(bf16[18,1,768]{2,1,0:T(2,128)(2,1)} %get-tuple-element.75), channel_id=1, source_target_pairs={{0,1},{1,2},{2,3},{3,4},{4,5},{5,6},{6,7},{8,9},{9,10},{10,11},{11... | collective-permute-start | bytes 82952 | tf_op jit(solution)/shard_map/ppermute | solution.py:25
  35.7 18.5 %copy-start.3 = (bf16[768,768]{1,0:T(8,128)(2,1)S(1)}, bf16[768,768]{1,0:T(8,128)(2,1)}, u32[]{:S(2)}) copy-start(bf16[768,768]{1,0:T(8,128)(2,1)} %param.10) | copy-start | bytes 3538948
  54.3 3.6 %copy-start.13 = (bf16[2,32,768]{2,1,0:T(8,128)(2,1)}, bf16[2,32,768]{2,1,0:T(8,128)(2,1)S(1)}, u32[]{:S(2)}) copy-start(bf16[2,32,768]{2,1,0:T(8,128)(2,1)S(1)} %copy.50) | copy-start | bytes 294916
  59.7 2.6 copy-start.15
  71.2 2.8 copy-start.9
  71.2 2.8 copy-start.14
  71.2 4.9 %copy-start.4 = (bf16[768,768]{1,0:T(8,128)(2,1)S(1)}, bf16[768,768]{1,0:T(8,128)(2,1)}, u32[]{:S(2)}) copy-start(bf16[768,768]{1,0:T(8,128)(2,1)} %param.11) | copy-start | bytes 3538948
  74.0 4.3 %copy-start.19 = (bf16[12,64,512]{2,1,0:T(8,128)(2,1)S(1)}, bf16[12,64,512]{2,1,0:T(8,128)(2,1)}, u32[]{:S(2)}) copy-start(bf16[12,64,512]{2,1,0:T(8,128)(2,1)} %convolution_convert_fusion.7) | copy-start | bytes 2359300
  74.0 4.3 %copy-start.34 = (bf16[16,32,768]{2,1,0:T(8,128)(2,1)S(1)}, bf16[16,32,768]{2,1,0:T(8,128)(2,1)}, u32[]{:S(2)}) copy-start(bf16[16,32,768]{2,1,0:T(8,128)(2,1)} %param.13) | copy-start | bytes 2359300
  78.0 104.2 %reduce-scatter.8.cloned.1.call-start = ((), (), s32[]{:S(2)}) async-start(), calls=%async_computation.4 | async-start | bytes 221184
  87.0 44.7 %copy-start.21 = (f32[2,4,768]{2,1,0:T(4,128)S(1)}, f32[2,4,768]{2,1,0:T(4,128)}, u32[]{:S(2)}) copy-start(f32[2,4,768]{2,1,0:T(4,128)} %copy-done.20) | copy-start | bytes 73732
  87.0 44.7 %copy-start.30 = (f32[2,4]{1,0:T(2,128)S(1)}, f32[2,4]{1,0:T(2,128)}, u32[]{:S(2)}) copy-start(f32[2,4]{1,0:T(2,128)} %copy-done.29) | copy-start | bytes 100
  87.1 44.7 %copy-start.32 = (f32[2,4]{1,0:T(2,128)S(1)}, f32[2,4]{1,0:T(2,128)}, u32[]{:S(2)}) copy-start(f32[2,4]{1,0:T(2,128)} %copy-done.31) | copy-start | bytes 100
  131.8 2.0 copy-start.18
  133.8 15.9 %copy-start.1 = (bf16[768,768]{0,1:T(8,128)(2,1)S(1)}, bf16[768,768]{0,1:T(8,128)(2,1)}, u32[]{:S(2)}) copy-start(bf16[768,768]{0,1:T(8,128)(2,1)} %convolution_convert_fusion.2) | copy-start | bytes 3538948
  133.8 15.9 %copy-start.2 = (bf16[768,768]{0,1:T(8,128)(2,1)S(1)}, bf16[768,768]{0,1:T(8,128)(2,1)}, u32[]{:S(2)}) copy-start(bf16[768,768]{0,1:T(8,128)(2,1)} %convolution_convert_fusion.3) | copy-start | bytes 3538948
  149.7 87.9 %reduce-scatter.6.cloned.1.call-start = ((), (), s32[]{:S(2)}) async-start(), calls=%async_computation.2 | async-start | bytes 5308416 | tf_op jit(solution)/shard_map/reduce_scatter | solution.py:202
  154.1 130.9 %all-reduce.4.cloned.1.call-start = ((), (), s32[]{:S(2)}) async-start(), calls=%async_computation.3 | async-start | bytes 1179648 | tf_op jit(solution)/shard_map/psum | solution.py:210
  155.2 6.0 %collective-permute-start.5 = (bf16[1,32,768]{2,1,0:T(8,128)(2,1)S(1)}, bf16[1,32,768]{2,1,0:T(8,128)(2,1)S(1)}, u32[]{:S(2)}, u32[]{:S(2)}) collective-permute-start(bf16[1,32,768]{2,1,0:T(8,128)(2,1)S(1)} %get-tuple-element.77), channel_id=1, source_target_pairs={{8,0},{16,8},{24,16},{9,1},{17,9},{25,17},{10,2},{18,10},{26,18},{... | collective-permute-start | bytes 147464 | tf_op jit(solution)/shard_map/ppermute | solution.py:27
  156.5 6.3 %collective-permute-start.4 = (bf16[1,32,768]{2,1,0:T(8,128)(2,1)S(1)}, bf16[1,32,768]{2,1,0:T(8,128)(2,1)S(1)}, u32[]{:S(2)}, u32[]{:S(2)}) collective-permute-start(bf16[1,32,768]{2,1,0:T(8,128)(2,1)S(1)} %get-tuple-element.76), channel_id=1, source_target_pairs={{0,8},{8,16},{16,24},{1,9},{9,17},{17,25},{2,10},{10,18},{18,26},{... | collective-permute-start | bytes 147464 | tf_op jit(solution)/shard_map/ppermute | solution.py:25
  162.9 74.8 %collective-permute-start.7 = (bf16[18,1,768]{2,1,0:T(2,128)(2,1)S(1)}, bf16[18,1,768]{2,1,0:T(2,128)(2,1)S(1)}, u32[]{:S(2)}, u32[]{:S(2)}) collective-permute-start(bf16[18,1,768]{2,1,0:T(2,128)(2,1)S(1)} %get-tuple-element.73), channel_id=1, source_target_pairs={{1,0},{2,1},{3,2},{4,3},{5,4},{6,5},{7,6},{9,8},{10,9},{11,10},{12... | collective-permute-start | bytes 82952 | tf_op jit(solution)/shard_map/ppermute | solution.py:27
  164.2 73.5 %collective-permute-start.6 = (bf16[18,1,768]{2,1,0:T(2,128)(2,1)S(1)}, bf16[18,1,768]{2,1,0:T(2,128)(2,1)S(1)}, u32[]{:S(2)}, u32[]{:S(2)}) collective-permute-start(bf16[18,1,768]{2,1,0:T(2,128)(2,1)S(1)} %get-tuple-element.72), channel_id=1, source_target_pairs={{0,1},{1,2},{2,3},{3,4},{4,5},{5,6},{6,7},{8,9},{9,10},{10,11},{11... | collective-permute-start | bytes 82952 | tf_op jit(solution)/shard_map/ppermute | solution.py:25
  (15 other events, 19.7 us)
Sparse Core Ops, SparseCore 0:
  78.2 53.5 all-reduce.5
  149.8 32.3 reduce-scatter.7
  184.5 53.0 reduce-scatter.5
  240.5 44.4 all-reduce.3
where the time goes:
time: 295 us; the launch traced here: 294 us
  waiting for transfers between devices  149 us (51%)
  matrix products  38.1 us (13%)
  local copies, waits for them, and re-layouts  29.3 us (10%)
  blocking collectives  23.8 us (8%)
  starting transfers between devices  21.6 us (7%)
  other arithmetic  16.9 us (6%)
  between operations  14.9 us (5%)
    unnamed x6, waiting for transfers between devices  57.7 us
    reduce_scatter x1, waiting for transfers between devices, on_device(): lax.psum_scatter(weight_terms.astype(jnp.bfloat16), 'col', scatter_dimens...  44.2 us
    psum x1, waiting for transfers between devices, on_device(): lax.psum(column_sums[0].astype(jnp.bfloat16), 'row').astype(jnp.float32)  43.3 us
    ppermute x4, starting transfers between devices, with_halo(): lax.ppermute(tail, axis, [(i, (i + 1) % count) for i in range(ends)])  16.1 us
    all_gather x1, blocking collectives, on_device(): gathered = lax.all_gather(normed, 'col', axis=1, tiled=True)  14 us
    psum x1, blocking collectives, on_device(): lax.psum(column_sums[1].astype(jnp.bfloat16), 'row').astype(jnp.float32)  9.8 us
    unnamed x76, local copies, waits for them, and re-layouts  9.51 us
    dot_general x2, matrix products, contract_last(): lax.dot_general(left, right, (((1,), (1,)), ((), ())), preferred_element_...  8.7 us
  transfers between devices with their start and end apart: 12, of which 7 were waited for; matrix products, arithmetic and copies ran while one was open for 8% of the time, Pallas kernels for 0%

commit v1 on v0

v1 whole, which is shorter than its diff:
```python
from functools import partial
import math

import jax
import jax.numpy as jnp
from jax import lax
from jax.experimental import pallas as pl
from jax.experimental.pallas import tpu as pltpu
from jax.sharding import PartitionSpec as P

HEADS = 12
HD = 64
POOL = 8


EPSILON = 1e-05


def contract_first(left, right):
    return lax.dot_general(
        left, right, (((0,), (0,)), ((), ())), preferred_element_type=jnp.float32
    )


def contract_last(left, right):
    return lax.dot_general(
        left, right, (((1,), (1,)), ((), ())), preferred_element_type=jnp.float32
    )


def stencil(padded, taps, height, width, flipped):
    total = jnp.zeros((height, width, padded.shape[2]), jnp.float32)
    for tap_row in range(3):
        for tap_col in range(3):
            if flipped:
                window = padded[
                    2 - tap_row : 2 - tap_row + height, 2 - tap_col : 2 - tap_col + width
                ]
            else:
                window = padded[tap_row : tap_row + height, tap_col : tap_col + width]
            total = total + taps[3 * tap_row + tap_col] * window.astype(jnp.float32)
    return total


def attend(carry, inputs, key_heads, value_heads):
    grad_key, grad_value = carry
    query_block, dout_block = inputs
    softmax_scale = HD ** (-0.5)
    query_heads = query_block.reshape(-1, HEADS, HD)
    dout_heads = dout_block.reshape(-1, HEADS, HD)
    scores = (
        jnp.einsum("qhd,khd->hqk", query_heads, key_heads, preferred_element_type=jnp.float32)
        * softmax_scale
    )
    expons = jnp.exp(scores)
    probabilities = expons / jnp.sum(expons, axis=-1, keepdims=True)
    weights = probabilities.astype(jnp.bfloat16)
    attended = jnp.einsum(
        "hqk,khd->qhd", weights, value_heads, preferred_element_type=jnp.float32
    ).astype(jnp.bfloat16)
    grad_probs = jnp.einsum(
        "qhd,khd->hqk", dout_heads, value_heads, preferred_element_type=jnp.float32
    )
    deltas = jnp.einsum("qhd,qhd->hq", dout_heads, attended, preferred_element_type=jnp.float32)
    grad_scores = (probabilities * (grad_probs - deltas[:, :, None]) * softmax_scale).astype(
        jnp.bfloat16
    )
    grad_query = jnp.einsum(
        "hqk,khd->qhd", grad_scores, key_heads, preferred_element_type=jnp.float32
    ).astype(jnp.bfloat16)
    grad_key = grad_key + jnp.einsum(
        "hqk,qhd->khd", grad_scores, query_heads, preferred_element_type=jnp.float32
    )
    grad_value = grad_value + jnp.einsum(
        "hqk,qhd->khd", weights, dout_heads, preferred_element_type=jnp.float32
    )
    return (
        (grad_key, grad_value),
        (attended.reshape(query_block.shape), grad_query.reshape(query_block.shape)),
    )


MESH = pl.DeviceIdType.MESH
VMEM = pl.BlockSpec(memory_space=pltpu.VMEM)
DIRECTIONS = ((-1, 0), (1, 0), (0, -1), (0, 1), (-1, -1), (-1, 1), (1, -1), (1, 1))


def remote(source, target, send, recv, row, col):
    return pltpu.make_async_remote_copy(
        src_ref=source,
        dst_ref=target,
        send_sem=send,
        recv_sem=recv,
        device_id=(row, col),
        device_id_type=MESH,
    )


def greet_line(barrier, row, col, count, along_row):
    for step in range(1, count):
        where = (lax.rem(row + step, count), col) if along_row else (row, lax.rem(col + step, count))
        pl.semaphore_signal(barrier, inc=1, device_id=where, device_id_type=MESH)


def halo_kernel(rows_n, cols_n, with_cells, *refs):
    if with_cells:
        rows, cols, corners, cells, out_rows, out_cols, out_corners, out_cells, send, recv, cell_send, cell_recv = refs
    else:
        rows, cols, corners, out_rows, out_cols, out_corners, send, recv = refs
    row, col = lax.axis_index("row"), lax.axis_index("col")
    sources = [rows.at[0], rows.at[1], cols.at[0], cols.at[1]] + [corners.at[i] for i in range(4)]
    targets = [out_rows.at[1], out_rows.at[0], out_cols.at[1], out_cols.at[0]]
    targets += [out_corners.at[3 - i] for i in range(4)]
    out_rows[...] = jnp.zeros_like(out_rows)
    out_cols[...] = jnp.zeros_like(out_cols)
    out_corners[...] = jnp.zeros_like(out_corners)

    def present(down, right):
        ok = None
        for move, at, count in ((down, row, rows_n), (right, col, cols_n)):
            if move == 0:
                continue
            here = at > 0 if move < 0 else at < count - 1
            ok = here if ok is None else jnp.logical_and(ok, here)
        return ok

    barrier = pltpu.get_barrier_semaphore()
    for down, right in DIRECTIONS:
        @pl.when(present(down, right))
        def _(down=down, right=right):
            pl.semaphore_signal(barrier, inc=1, device_id=(row + down, col + right), device_id_type=MESH)
    if with_cells:
        greet_line(barrier, row, col, cols_n, False)
    greeted = sum(present(down, right).astype(jnp.int32) for down, right in DIRECTIONS)
    pl.semaphore_wait(barrier, greeted + (cols_n - 1 if with_cells else 0))

    def edge(at):
        down, right = DIRECTIONS[at]
        return remote(sources[at], targets[at], send.at[at], recv.at[at], row + down, col + right)

    def cell(step):
        return remote(cells, out_cells.at[col], cell_send.at[step], cell_recv.at[step], row, lax.rem(col + step, cols_n))

    for at, (down, right) in enumerate(DIRECTIONS):
        @pl.when(present(down, right))
        def _(at=at):
            edge(at).start()
    if with_cells:
        out_cells[col] = cells[...]
        for step in range(1, cols_n):
            cell(step).start()
    for at, (down, right) in enumerate(DIRECTIONS):
        @pl.when(present(down, right))
        def _(at=at):
            edge(at).wait_send()

        @pl.when(present(-down, -right))
        def _(at=at):
            edge(at).wait_recv()
    if with_cells:
        for step in range(1, cols_n):
            cell(step).wait()


def halo_exchange(tile, rows_n, cols_n, identity, cells=None):
    height, width, channels = tile.shape
    rows = jnp.stack([tile[0], tile[-1]])
    cols = jnp.stack([tile[:, 0], tile[:, -1]])
    corners = jnp.broadcast_to(
        jnp.stack([tile[0, 0], tile[0, -1], tile[-1, 0], tile[-1, -1]])[:, None], (4, 16, channels)
    )
    operands = [rows, cols, corners]
    scratch = [pltpu.SemaphoreType.DMA((8,)), pltpu.SemaphoreType.DMA((8,))]
    shapes = [jax.ShapeDtypeStruct(x.shape, x.dtype) for x in operands]
    if cells is not None:
        operands.append(cells)
        shapes.append(jax.ShapeDtypeStruct((cols_n,) + cells.shape, cells.dtype))
        scratch += [pltpu.SemaphoreType.DMA((cols_n,)), pltpu.SemaphoreType.DMA((cols_n,))]
    got = pl.pallas_call(
        partial(halo_kernel, rows_n, cols_n, cells is not None),
        out_shape=shapes,
        in_specs=[VMEM] * len(operands),
        out_specs=[VMEM] * len(shapes),
        scratch_shapes=scratch,
        compiler_params=pltpu.CompilerParams(collective_id=identity, has_side_effects=True),
    )(*operands)
    out_rows, out_cols, out_corners = got[:3]
    def band(at, left, right):
        return jnp.concatenate([left[None, :1], out_rows[at][None], right[None, :1]], axis=1)
    middle = jnp.concatenate([out_cols[0][:, None], tile, out_cols[1][:, None]], axis=1)
    padded = jnp.concatenate(
        [band(0, out_corners[0], out_corners[1]), middle, band(1, out_corners[2], out_corners[3])], axis=0
    )
    return padded if cells is None else (padded, got[3])


def gather_kernel(cols_n, block, out, send, recv):
    row, col = lax.axis_index("row"), lax.axis_index("col")
    barrier = pltpu.get_barrier_semaphore()
    greet_line(barrier, row, col, cols_n, False)
    pl.semaphore_wait(barrier, cols_n - 1)
    copies = [
        remote(block, out.at[col], send.at[step], recv.at[step], row, lax.rem(col + step, cols_n))
        for step in range(1, cols_n)
    ]
    for copy in copies:
        copy.start()
    out[col] = block[...]
    for copy in copies:
        copy.wait()


def gather_cells(block, cols_n, identity):
    return pl.pallas_call(
        partial(gather_kernel, cols_n),
        out_shape=jax.ShapeDtypeStruct((cols_n,) + block.shape, block.dtype),
        in_specs=[VMEM],
        out_specs=VMEM,
        scratch_shapes=[pltpu.SemaphoreType.DMA((cols_n,)), pltpu.SemaphoreType.DMA((cols_n,))],
        compiler_params=pltpu.CompilerParams(collective_id=identity, has_side_effects=True),
    )(block)


def scatter_kernel(cols_n, blocks, out, landed, send, recv):
    row, col = lax.axis_index("row"), lax.axis_index("col")
    barrier = pltpu.get_barrier_semaphore()
    greet_line(barrier, row, col, cols_n, False)
    pl.semaphore_wait(barrier, cols_n - 1)
    copies = []
    for step in range(1, cols_n):
        owner = lax.rem(col + step, cols_n)
        copies.append(remote(blocks.at[owner], landed.at[step], send.at[step], recv.at[step], row, owner))
    for copy in copies:
        copy.start()
    total = blocks[col].astype(jnp.float32)
    for step, copy in enumerate(copies):
        copy.wait()
        total = total + landed[step + 1].astype(jnp.float32)
    out[...] = total


def scatter_sum(blocks, cols_n, identity):
    return pl.pallas_call(
        partial(scatter_kernel, cols_n),
        out_shape=jax.ShapeDtypeStruct(blocks.shape[1:], jnp.float32),
        in_specs=[VMEM],
        out_specs=VMEM,
        scratch_shapes=[
            pltpu.VMEM(blocks.shape, blocks.dtype),
            pltpu.SemaphoreType.DMA((cols_n,)),
            pltpu.SemaphoreType.DMA((cols_n,)),
        ],
        compiler_params=pltpu.CompilerParams(collective_id=identity, has_side_effects=True),
    )(blocks)


def reduce_kernel(
    rows_n, cols_n, terms, cells, taps, out, out_cells, out_taps,
    landed1, held1, landed2, held2, landed3, taps1, taps_held, taps2,
    send1, recv1, send2, recv2, send3, recv3, send4, recv4, send_cells, recv_cells,
    send_t1, recv_t1, send_t2, recv_t2,
):
    row, col = lax.axis_index("row"), lax.axis_index("col")
    chip, core = col // 2, lax.rem(col, 2)
    chips = cols_n // 2
    items = cols_n // 4
    half = items // 2
    is_cells = jnp.logical_and(chip >= half, chip < chips - half)
    is_terms = jnp.logical_or(chip < half, chip >= chips - half)
    barrier = pltpu.get_barrier_semaphore()
    greet_line(barrier, row, col, cols_n, False)
    greet_line(barrier, row, col, rows_n, True)
    pl.semaphore_wait(barrier, cols_n + rows_n - 2)

    def mate(step):
        return lax.rem(row + step, rows_n)

    def first(item):
        return remote(
            terms.at[1 - core, item], landed1.at[item], send1.at[item], recv1.at[item], row, 2 * chip + 1 - core
        )

    def second(item, step):
        return remote(
            held1.at[item, mate(step)], landed2.at[item, step - 1], send2.at[item, step - 1],
            recv2.at[item, step - 1], mate(step), col,
        )

    def owner_of(item):
        return item if item < half else chips - items + item

    def third(item):
        return remote(
            held2.at[item], landed3.at[chip], send3.at[item], recv3.at[chip], row, 2 * owner_of(item) + core
        )

    def fourth(step):
        return remote(out.at[row], out.at[row], send4.at[step - 1], recv4.at[step - 1], mate(step), col)

    def cell(step):
        return remote(
            cells, out_cells.at[row], send_cells.at[step - 1], recv_cells.at[step - 1], mate(step), col
        )

    def tap_first(step):
        owner = lax.rem(col + step, cols_n)
        return remote(taps.at[owner], taps1.at[step - 1], send_t1.at[step - 1], recv_t1.at[step - 1], row, owner)

    def tap_second(step):
        return remote(taps_held, taps2.at[step - 1], send_t2.at[step - 1], recv_t2.at[step - 1], mate(step), col)

    for item in range(items):
        first(item).start()
    for step in range(1, cols_n):
        tap_first(step).start()
    for item in range(items):
        first(item).wait_recv()
        for step in range(1, rows_n + 1):
            there = mate(step)
            held1[item, there] = (
                terms[core, item, there].astype(jnp.float32) + landed1[item, there].astype(jnp.float32)
            ).astype(held1.dtype)
            if step < rows_n:
                second(item, step).start()

    @pl.when(is_cells)
    def _():
        for step in range(1, rows_n):
            cell(step).start()

    out_cells[row] = cells[...]
    tap_total = taps[col].astype(jnp.float32)
    for step in range(1, cols_n):
        tap_first(step).wait_recv()
        tap_total = tap_total + taps1[step - 1].astype(jnp.float32)
    taps_held[...] = tap_total.astype(taps_held.dtype)
    for step in range(1, rows_n):
        tap_second(step).start()
    for item in range(items):
        total = held1[item, row].astype(jnp.float32)
        for step in range(1, rows_n):
            second(item, step).wait_recv()
            total = total + landed2[item, step - 1].astype(jnp.float32)
        held2[item] = total.astype(held2.dtype)

        @pl.when(chip != owner_of(item))
        def _(item=item):
            third(item).start()

    tap_total = taps_held[...].astype(jnp.float32)
    for step in range(1, rows_n):
        tap_second(step).wait_recv()
        tap_total = tap_total + taps2[step - 1].astype(jnp.float32)
    out_taps[...] = tap_total

    @pl.when(is_terms)
    def _():
        mine = lax.rem(chip, chips - items)
        total = held2[mine].astype(jnp.float32)
        for step in range(1, chips):
            source = lax.rem(chip + step, chips)
            remote(
                held2.at[0], landed3.at[source], send3.at[0], recv3.at[source], row, 2 * source + core
            ).wait_recv()
            total = total + landed3[source].astype(jnp.float32)
        out[row] = total.astype(out.dtype)
        for step in range(1, rows_n):
            fourth(step).start()
        for step in range(1, rows_n):
            fourth(step).wait()

    @pl.when(is_cells)
    def _():
        for step in range(1, rows_n):
            cell(step).wait()

    for item in range(items):
        first(item).wait_send()
        for step in range(1, rows_n):
            second(item, step).wait_send()

        @pl.when(chip != owner_of(item))
        def _(item=item):
            third(item).wait_send()

    for step in range(1, cols_n):
        tap_first(step).wait_send()
    for step in range(1, rows_n):
        tap_second(step).wait_send()


def reduce_all(terms, cells, taps, rows_n, cols_n, identity):
    _, items, _, high, wide = terms.shape
    chips = cols_n // 2
    kind = terms.dtype
    def sems(*shape):
        return [pltpu.SemaphoreType.DMA(shape), pltpu.SemaphoreType.DMA(shape)]
    return pl.pallas_call(
        partial(reduce_kernel, rows_n, cols_n),
        out_shape=[
            jax.ShapeDtypeStruct((rows_n, high, wide), kind),
            jax.ShapeDtypeStruct((rows_n,) + cells.shape, kind),
            jax.ShapeDtypeStruct(taps.shape[1:], jnp.float32),
        ],
        in_specs=[VMEM] * 3,
        out_specs=[VMEM] * 3,
        scratch_shapes=[
            pltpu.VMEM((items, rows_n, high, wide), kind),
            pltpu.VMEM((items, rows_n, high, wide), kind),
            pltpu.VMEM((items, rows_n - 1, high, wide), kind),
            pltpu.VMEM((items, high, wide), kind),
            pltpu.VMEM((chips, high, wide), kind),
            pltpu.VMEM((cols_n - 1,) + taps.shape[1:], kind),
            pltpu.VMEM(taps.shape[1:], kind),
            pltpu.VMEM((rows_n - 1,) + taps.shape[1:], kind),
        ]
        + sems(items)
        + sems(items, rows_n - 1)
        + [pltpu.SemaphoreType.DMA((items,)), pltpu.SemaphoreType.DMA((chips,))]
        + sems(rows_n - 1)
        + sems(rows_n - 1)
        + sems(cols_n - 1)
        + sems(rows_n - 1),
        compiler_params=pltpu.CompilerParams(collective_id=identity, has_side_effects=True),
    )(terms, cells, taps)


def split_terms(query_terms, out_terms, rows_n, cols_n, shard):
    parts = []
    for core in range(2):
        for term in (query_terms, out_terms):
            for item in range(cols_n // 8):
                at = (2 * item + core) * shard
                parts.append(term[:, at : at + shard])
    stacked = jnp.stack(parts)
    return stacked.reshape(2, cols_n // 4, rows_n, query_terms.shape[0] // rows_n, shard)


def on_device(image, conv_taps, w_query, w_key, w_value, w_out, grad_out):
    rows_n, cols_n = lax.axis_size("row"), lax.axis_size("col")
    height, width, channels = image.shape
    padded = halo_exchange(image, rows_n, cols_n, 0)
    mixed = image.astype(jnp.float32) + stencil(padded, conv_taps, height, width, False)
    hidden = mixed.astype(jnp.bfloat16)
    flat_hidden = hidden.reshape(-1, channels)
    query = jnp.dot(flat_hidden, w_query, preferred_element_type=jnp.float32).astype(jnp.bfloat16)
    pooled = (
        hidden.astype(jnp.float32)
        .reshape(height // POOL, POOL, width // POOL, POOL, channels)
        .mean(axis=(1, 3))
    )
    centre = jnp.mean(pooled, axis=-1, keepdims=True)
    spread = jnp.mean(jnp.square(pooled - centre), axis=-1, keepdims=True)
    inverse = lax.rsqrt(spread + EPSILON)
    standard = (pooled - centre) * inverse
    own_cells = standard.astype(jnp.bfloat16).reshape(-1, channels)
    own = own_cells.shape[0]
    key_cells = gather_cells(own_cells, cols_n, 1).reshape(-1, channels)
    keys = jnp.dot(key_cells, w_key, preferred_element_type=jnp.float32).astype(jnp.bfloat16)
    values = jnp.dot(key_cells, w_value, preferred_element_type=jnp.float32).astype(jnp.bfloat16)
    flat_grad = grad_out.reshape(-1, channels)
    dout = contract_last(flat_grad, w_out).astype(jnp.bfloat16)
    key_heads = keys.reshape(-1, HEADS, HD)
    value_heads = values.reshape(-1, HEADS, HD)
    empty_grad = jnp.zeros(key_heads.shape, jnp.float32)
    (grad_key, grad_value), (attended, grad_query) = attend(
        (empty_grad, empty_grad), (query, dout), key_heads, value_heads
    )
    grad_wout = contract_first(attended, flat_grad)
    grad_wquery = contract_first(flat_hidden, grad_query)
    grad_hidden = contract_last(grad_query, w_query)
    cell_grads = jnp.concatenate(
        [grad_key.reshape(cols_n, own, channels), grad_value.reshape(cols_n, own, channels)], axis=1
    ).astype(jnp.bfloat16)
    totals = scatter_sum(cell_grads, cols_n, 2)
    sent_totals = totals.astype(jnp.bfloat16)
    rest = (totals - sent_totals.astype(jnp.float32)).astype(jnp.bfloat16)
    def exact(at, weight):
        both = jnp.concatenate([sent_totals[at : at + own], rest[at : at + own]], axis=0)
        product = contract_last(both, weight)
        return product[:own] + product[own:]
    grad_normed = (exact(0, w_key) + exact(own, w_value)).reshape(standard.shape)
    grad_pooled = (
        grad_normed
        - jnp.mean(grad_normed, axis=-1, keepdims=True)
        - standard * jnp.mean(grad_normed * standard, axis=-1, keepdims=True)
    ) * inverse
    spread_back = jnp.broadcast_to(
        (grad_pooled / (POOL * POOL))[:, None, :, None, :],
        (height // POOL, POOL, width // POOL, POOL, channels),
    ).reshape(height, width, channels)
    grad_mixed = (
        grad_out.astype(jnp.float32) + grad_hidden.reshape(height, width, channels) + spread_back
    )
    grad_padded, all_totals = halo_exchange(
        grad_mixed.astype(jnp.bfloat16), rows_n, cols_n, 3, sent_totals
    )
    grad_image = (grad_mixed + stencil(grad_padded, conv_taps, height, width, True)).astype(
        jnp.bfloat16
    )
    tap_list = []
    for tap_row in range(3):
        for tap_col in range(3):
            window = padded[tap_row : tap_row + height, tap_col : tap_col + width].astype(
                jnp.float32
            )
            tap_list.append(jnp.sum(grad_mixed * window, axis=(0, 1)))
    tap_terms = jnp.stack(tap_list, axis=0)
    tap_terms = jnp.pad(tap_terms, ((0, 16 - tap_terms.shape[0]), (0, 0))).astype(jnp.bfloat16)
    tap_terms = tap_terms.reshape(16, cols_n, -1).transpose(1, 0, 2)
    shard = 4 * channels // cols_n
    quarter = cols_n // 4
    col = lax.axis_index("col")
    terms = split_terms(
        grad_wquery.astype(jnp.bfloat16), grad_wout.astype(jnp.bfloat16), rows_n, cols_n, shard
    )
    side = jnp.where(
        col < 2 * quarter,
        all_totals[:, :own].reshape(-1, channels),
        all_totals[:, own:].reshape(-1, channels),
    )
    mine = lax.dynamic_slice_in_dim(side, lax.rem(col, quarter) * shard, shard, axis=1)
    cells = jnp.concatenate([key_cells, mine], axis=1)
    summed, gathered, grad_conv = reduce_all(terms, cells, tap_terms, rows_n, cols_n, 4)
    gathered = gathered.reshape(-1, channels + shard)
    from_cells = contract_first(gathered[:, :channels], gathered[:, channels:])
    is_cells = jnp.logical_and(col >= quarter, col < cols_n - quarter)
    grad_weights = jnp.where(
        is_cells, from_cells, summed.reshape(channels, shard).astype(jnp.float32)
    )
    return (grad_image, grad_weights, grad_conv[:9])


def solution(mesh):
    return jax.shard_map(
        on_device,
        mesh=mesh,
        in_specs=(P("row", "col", None), P(), P(), P(), P(), P(), P("row", "col", None)),
        out_specs=(P("row", "col", None), P(None, "col"), P(None, "col")),
        check_vma=False,
    )
```

time: 295 us -> 173 us (0.59)
  the two profiles are of different devices: /device:TPU:0 before, /device:TPU:24 now
where the time goes in v1:
time: 173 us; the launch traced here: 171 us
  Pallas kernels  78 us (45%)
  local copies, waits for them, and re-layouts  41.5 us (24%)
  matrix products  33 us (19%)
  other arithmetic  17.2 us (10%)
    pallas_call x1, Pallas kernels, reduce_all(): pl.pallas_call(partial(reduce_kernel, rows_n, cols_n), out_shape=[jax.Sha...  41.4 us
    pallas_call x2, Pallas kernels, halo_exchange(): pl.pallas_call(partial(halo_kernel, rows_n, cols_n, cells is not None), o...  18.6 us
    dot_general x4, matrix products, contract_last(): lax.dot_general(left, right, (((1,), (1,)), ((), ())), preferred_element_...  9.75 us
    pallas_call x1, Pallas kernels, scatter_sum(): pl.pallas_call(partial(scatter_kernel, cols_n), out_shape=jax.ShapeDtypeS...  9.38 us
    dot_general x2, local copies, waits for them, and re-layouts, contract_last(): lax.dot_general(left, right, (((1,), (1,)), ((), ())), preferred_element_...  8.93 us
    pallas_call x1, Pallas kernels, gather_cells(): pl.pallas_call(partial(gather_kernel, cols_n), out_shape=jax.ShapeDtypeSt...  8.58 us
    dot_general x3, matrix products, contract_first(): lax.dot_general(left, right, (((0,), (0,)), ((), ())), preferred_element_...  6.85 us
    unnamed x95, local copies, waits for them, and re-layouts  4.76 us

profile of v1, /device:TPU:24, one launch (start us, length us, event | category | flops | bytes accessed | tf_op | source)
XLA Modules:
  0.0 171.1 jit_solution(16742304371469641342)
XLA Ops:
  1.6 1.7 %slice_reduce_fusion.8 = (f32[768]{0:T(1024)S(1)}, f32[768]{0:T(1024)S(1)}, f32[768]{0:T(1024)S(1)}, f32[768]{0:T(1024)S(1)}, f32[768]{0:T(1024)}, /*index=5*/f3...) fusion(f32[9,768]{1,0:T(8,128)} %param.8), kind=kLoop, calls=%fused_computation.139 | loop fusion | bytes 55296 | tf_op jit(solution)/shard_map/slice | solution.py:41
  5.4 1.6 copy.118
  7.7 8.4 %shard_map.94 = (bf16[2,32,768]{2,1,0:T(8,128)(2,1)}, bf16[2,16,768]{2,1,0:T(8,128)(2,1)}, bf16[4,16,768]{2,1,0:T(8,128)(2,1)}) custom-call(bf16[2,32,768]{2,1,0:T(8,128)(2,1)} %pad_maximum_fusion.7.refs_0_, bf16[2,16,768]{2,1,0:T(8,128)(2,1)} %pad_maximum_fusion.9.refs_1_, bf16[4,16,768]{2,1,0:T(8,128)(2,1)} %broadcast_in_dim.6.refs_2_), custom_call_target="tpu_custom_call" | custom-call | tf_op jit(solution)/shard_map/pallas_call | solution.py:179
  17.7 1.4 slice_bitcast_fusion.11
  20.9 2.1 %convolution_convert_fusion.2 = bf16[512,768]{1,0:T(8,128)(2,1)S(1)} fusion(bf16[512,768]{1,0:T(8,128)(2,1)S(1)} %bitcast.142, bf16[768,768]{1,0:T(8,128)(2,1)} %param.12), kind=kOutput, calls=%fused_computation.49 | convolution fusion | flops 604372992 | bytes 2752512 | tf_op jit(solution)/shard_map/dot_general | solution.py:26
  23.3 1.9 %maximum_maximum_fusion = (bf16[17,34,768]{2,0,1:T(8,128)(2,1)S(1)}, bf16[17,34,768]{2,0,1:T(8,128)(2,1)S(1)}) fusion(bf16[16,1,768]{2,0,1:T(8,128)(2,1)} %get-tuple-element.103, bf16[16,32,768]{2,0,1:T(8,128)(2,1)S(1)} %copy.118, bf16[16,1,768]{2,0,1:T(8,128)(2,1)} %get-tuple-element.102, bf16[1,1,768]{2,0,1:T(2,128)(2,1)} %get-tuple-element.97, ...), kind=kLoop, calls=%fused_computation.53 | loop fusion | flops 10653696 | bytes 2715648 | tf_op jit(solution)/shard_map/concatenate | solution.py:191
  25.3 2.0 %fusion.18 = bf16[16,32,768]{2,0,1:T(8,128)(2,1)S(1)} fusion(bf16[16,32,768]{2,0,1:T(8,128)(2,1)S(1)} %copy.118, bf16[16,1,768]{2,0,1:T(8,128)(2,1)S(1)} %copy-done.20, bf16[16,1,768]{2,0,1:T(8,128)(2,1)S(1)} %copy-done.18, f32[768]{0:T(1024)S(1)} %copy-done.33, f32[768]{0:T(1024)S(1)} %copy-done.35, f32[768]{0:T(1024)S(1)} %get-tuple-element.50, ...), kind=kLoop, calls=%fused_computation.44 | loop fusion | flops 11796480 | bytes 6368256 | tf_op jit(solution)/shard_map/convert_element_type | solution.py:444
  29.0 8.6 %shard_map.95 = bf16[8,8,768]{2,1,0:T(8,128)(2,1)} custom-call(bf16[8,768]{1,0:T(8,128)(2,1)} %fusion.47.block), custom_call_target="tpu_custom_call" | custom-call | tf_op jit(solution)/shard_map/pallas_call | solution.py:214
  37.6 1.7 convolution_convert_fusion.9
  40.1 1.6 convolution_convert_fusion.8
  44.8 1.8 %fusion.28 = f32[12,512,64]{1,2,0:T(8,128)S(1)} fusion(bf16[64,12,64]{0,2,1:T(8,128)(2,1)} %bitcast.134, bf16[512,12,64]{0,2,1:T(8,128)(2,1)} %bitcast.125), kind=kOutput, calls=%fused_computation.71 | convolution fusion | flops 51124288 | bytes 2457600 | tf_op jit(solution)/shard_map/div | solution.py:56
  47.6 1.9 %copy.143 = bf16[64,12,64]{2,1,0:T(8,128)(2,1)} copy(bf16[64,12,64]{0,2,1:T(8,128)(2,1)} %fusion.22) | data formatting | bytes 196608 | tf_op jit(solution)/shard_map/hqk,qhd->khd/transpose | solution.py:74
  49.5 1.7 %reshape.179 = bf16[8,8,768]{2,1,0:T(8,128)(2,1)} reshape(bf16[64,12,64]{2,1,0:T(8,128)(2,1)} %copy.143) | data formatting | bytes 196608 | tf_op jit(solution)/shard_map/reshape | solution.py:473
  51.2 1.3 convolution_convert_fusion.5
  52.6 1.8 %convolution_convert_fusion = bf16[768,768]{1,0:T(8,128)(2,1)} fusion(bf16[512,768]{0,1:T(8,128)(2,1)S(1)} %bitcast.133, bf16[512,768]{1,0:T(8,128)(2,1)S(1)} %bitcast.143), kind=kOutput, calls=%fused_computation.45 | convolution fusion | flops 604569600 | bytes 2752512 | tf_op jit(solution)/shard_map/dot_general | solution.py:20
  54.4 1.6 fusion.69
  56.0 3.2 %fusion.21 = bf16[64,12,64]{0,2,1:T(8,128)(2,1)} fusion(bf16[512,12,64]{0,2,1:T(8,128)(2,1)} %bitcast.126, f32[12,512,64]{1,2,0:T(8,128)S(1)} %fusion.28, f32[12,512,64]{1,2,0:T(8,128)} %fusion.69, bf16[12,512,64]{1,2,0:T(8,128)(2,1)S(1)} %bitcast.122, bf16[12,64,512]{2,1,0:T(8,128)(2,1)} %copy-done.14), kind=kOutput, calls=%fused_computation.60 | convolution fusion | flops 53139520 | bytes 5603328 | tf_op jit(solution)/shard_map/hqk,qhd->khd/dot_general | solution.py:71
  59.2 3.3 %convolution_convert_fusion.4 = bf16[12,64,512]{2,1,0:T(8,128)(2,1)} fusion(bf16[64,12,64]{0,2,1:T(8,128)(2,1)} %bitcast.135, f32[12,512,64]{1,2,0:T(8,128)S(1)} %fusion.28, f32[12,512,64]{1,2,0:T(8,128)} %fusion.69, bf16[12,512,64]{1,2,0:T(8,128)(2,1)S(1)} %bitcast.123, bf16[12,64,512]{2,1,0:T(8,128)(2,1)} %copy-done.14), kind=kOutput, calls=%fused_computation.51 | convolution fusion | flops 53483584 | bytes 5603328 | tf_op jit(solution)/shard_map/hqk,khd->qhd/dot_general | solution.py:68
  62.5 2.0 %copy.142 = bf16[64,12,64]{2,1,0:T(8,128)(2,1)} copy(bf16[64,12,64]{0,2,1:T(8,128)(2,1)} %fusion.21) | data formatting | bytes 196608 | tf_op jit(solution)/shard_map/hqk,qhd->khd/transpose | solution.py:71
  64.5 1.7 %reshape.178 = bf16[8,8,768]{2,1,0:T(8,128)(2,1)} reshape(bf16[64,12,64]{2,1,0:T(8,128)(2,1)} %copy.142) | data formatting | bytes 196608 | tf_op jit(solution)/shard_map/reshape | solution.py:473
  66.3 1.6 pad_maximum_fusion.5.blocks
  67.9 9.4 %shard_map.96 = f32[16,768]{1,0:T(8,128)} custom-call(bf16[8,16,768]{2,1,0:T(8,128)(2,1)} %pad_maximum_fusion.5.blocks), custom_call_target="tpu_custom_call" | custom-call | tf_op jit(solution)/shard_map/pallas_call | solution.py:243
  81.2 2.3 %convolution_convert_fusion.1 = bf16[768,768]{1,0:T(8,128)(2,1)S(1)} fusion(bf16[512,768]{1,0:T(8,128)(2,1)} %bitcast.137, bf16[512,768]{0,1:T(8,128)(2,1)} %bitcast.127), kind=kOutput, calls=%fused_computation.46 | convolution fusion | flops 604569600 | bytes 2752512 | tf_op jit(solution)/shard_map/dot_general | solution.py:20
  83.7 1.8 %pad_maximum_fusion = bf16[4,768,384]{2,1,0:T(8,128)(2,1)} fusion(bf16[1,768,384]{2,1,0:T(8,128)(2,1)S(1)} %get-tuple-element.67, bf16[1,768,384]{2,1,0:T(8,128)(2,1)S(1)} %get-tuple-element.113, bf16[1,768,384]{2,1,0:T(8,128)(2,1)S(1)} %get-tuple-element.66, bf16[1,768,384]{2,1,0:T(8,128)(2,1)S(1)} %get-tuple-element.114), kind=kLoop, calls=%fused_computation.4 | loop fusion | flops 3538944 | bytes 4718592 | tf_op jit(solution)/shard_map/stack | solution.py:435
  85.5 1.4 broadcast_in_dim.7
  86.9 3.1 %reshape.194 = bf16[16,32,768]{1,0,2:T(8,128)(2,1)} reshape(bf16[512,12,64]{0,2,1:T(8,128)(2,1)S(1)} %bitcast.128) | data formatting | bytes 1572864 | tf_op jit(solution)/shard_map/dot_general | solution.py:26
  90.1 5.8 %copy.162 = bf16[16,32,768]{2,0,1:T(8,128)(2,1)} copy(bf16[16,32,768]{1,0,2:T(8,128)(2,1)} %reshape.194) | data formatting | bytes 1572864 | tf_op jit(solution)/shard_map/dot_general | solution.py:26
  95.9 6.8 %fusion.16 = (bf16[768]{0:T(1024)(128)(2,1)S(1)}, bf16[768]{0:T(1024)(128)(2,1)S(1)}, bf16[768]{0:T(1024)(128)(2,1)S(1)}, bf16[768]{0:T(1024)(128)(2,1)S(1)}, bf...) fusion(bf16[17,34,768]{2,0,1:T(8,128)(2,1)} %copy-done.3, ...), kind=kOutput, calls=%fused_computation.36 | convolution fusion | flops 618521856 | bytes 13039104 | tf_op jit(solution)/shard_map/dot_general | solution.py:26
  108.6 10.2 %shard_map.97 = (bf16[2,32,768]{2,1,0:T(8,128)(2,1)}, bf16[2,16,768]{2,1,0:T(8,128)(2,1)}, bf16[4,16,768]{2,1,0:T(8,128)(2,1)}, bf16[8,16,768]{2,1,0:T(8,128)(2,1)}) custom-call(bf16[2,32,768]{2,1,0:T(8,128)(2,1)} %copy.147.refs_0_, bf16[2,16,768]{2,1,0:T(8,128)(2,1)} %pad_maximum_fusion.10.refs_1_, bf16[4,16,768]{2,1,0:T(8,128)(2,1)} %broadcast_in_dim.8.refs_2_, ...), custom_call_target="tpu_custom_call" | custom-call | tf_op jit(solution)/shard_map/pallas_call | solution.py:179
  121.2 41.4 %shard_map.98 = (bf16[4,192,384]{2,1,0:T(8,128)(2,1)}, bf16[4,64,1152]{2,1,0:T(8,128)(2,1)}, f32[16,96]{1,0:T(8,128)}) custom-call(bf16[2,2,4,192,384]{4,3,2,1,0:T(8,128)(2,1)} %bitcast.119, bf16[64,1152]{1,0:T(8,128)(2,1)} %pad_maximum_fusion.6.cells, bf16[8,16,96]{2,1,0:T(8,128)(2,1)} %bitcast.140), custom_call_target="tpu_custom_call" | custom-call | tf_op jit(solution)/shard_map/pallas_call | solution.py:398
  162.6 2.8 %convolution_select_fusion = f32[768,384]{1,0:T(8,128)} fusion(bf16[768,384]{1,0:T(8,128)(2,1)} %bitcast.138, pred[]{:T(512)S(6)} %and.5, bf16[256,1152]{1,0:T(8,128)(2,1)} %bitcast.139), kind=kOutput, calls=%fused_computation.48 | convolution fusion | flops 151584768 | bytes 2359297 | tf_op jit(solution)/shard_map/dot_general | solution.py:20
  167.2 2.1 %add_convert_fusion = bf16[16,32,768]{2,0,1:T(8,128)(2,1)S(1)} fusion(f32[16,32,768]{2,0,1:T(8,128)S(1)} %copy-done.11, bf16[16,32,768]{2,0,1:T(8,128)(2,1)S(1)} %copy-done.8, bf16[17,34,768]{2,0,1:T(8,128)(2,1)S(1)} %get-tuple-element.69, bf16[16,1,768]{2,0,1:T(8,128)(2,1)S(1)} %get-tuple-element.100, bf16[16,1,768]{2,0,1:T(8,128)(2,1)S(1)} %get-tuple-element.101, ...), kind=kLoop, calls=%fused_computation.40 | loop fusion | flops 11796480 | bytes 7941120 | tf_op jit(solution)/shard_map/convert_element_type | solution.py:498
  (168 shorter events, 29.6 us)
Async XLA Ops:
  0.6 42.1 %copy-start = (bf16[768,768]{1,0:T(8,128)(2,1)S(1)}, bf16[768,768]{1,0:T(8,128)(2,1)}, u32[]{:S(2)}) copy-start(bf16[768,768]{1,0:T(8,128)(2,1)} %param.9) | copy-start | bytes 3538948
  4.7 16.1 %copy-start.44 = (bf16[16,32,768]{2,1,0:T(8,128)(2,1)S(1)}, bf16[16,32,768]{2,1,0:T(8,128)(2,1)}, u32[]{:S(2)}) copy-start(bf16[16,32,768]{2,1,0:T(8,128)(2,1)} %param.13) | copy-start | bytes 2359300
  7.0 18.3 %copy-start.4 = (bf16[16,32,768]{2,0,1:T(8,128)(2,1)}, bf16[16,32,768]{2,0,1:T(8,128)(2,1)S(1)}, u32[]{:S(2)}) copy-start(bf16[16,32,768]{2,0,1:T(8,128)(2,1)S(1)} %copy.118) | copy-start | bytes 2359300
  23.2 2.0 %copy-start.18 = (bf16[16,1,768]{2,0,1:T(8,128)(2,1)S(1)}, bf16[16,1,768]{2,0,1:T(8,128)(2,1)}, u32[]{:S(2)}) copy-start(bf16[16,1,768]{2,0,1:T(8,128)(2,1)} %get-tuple-element.102) | copy-start | bytes 73732
  23.3 2.0 %copy-start.20 = (bf16[16,1,768]{2,0,1:T(8,128)(2,1)S(1)}, bf16[16,1,768]{2,0,1:T(8,128)(2,1)}, u32[]{:S(2)}) copy-start(bf16[16,1,768]{2,0,1:T(8,128)(2,1)} %get-tuple-element.103) | copy-start | bytes 73732
  23.3 2.0 %copy-start.27 = (f32[768]{0:T(1024)S(1)}, f32[768]{0:T(1024)}, u32[]{:S(2)}) copy-start(f32[768]{0:T(1024)} %get-tuple-element.53) | copy-start | bytes 9220
  23.3 2.0 %copy-start.29 = (f32[768]{0:T(1024)S(1)}, f32[768]{0:T(1024)}, u32[]{:S(2)}) copy-start(f32[768]{0:T(1024)} %get-tuple-element.54) | copy-start | bytes 9220
  23.3 2.0 %copy-start.31 = (f32[768]{0:T(1024)S(1)}, f32[768]{0:T(1024)}, u32[]{:S(2)}) copy-start(f32[768]{0:T(1024)} %get-tuple-element.55) | copy-start | bytes 9220
  23.3 2.0 %copy-start.33 = (f32[768]{0:T(1024)S(1)}, f32[768]{0:T(1024)}, u32[]{:S(2)}) copy-start(f32[768]{0:T(1024)} %get-tuple-element.56) | copy-start | bytes 9220
  23.3 2.0 %copy-start.35 = (f32[768]{0:T(1024)S(1)}, f32[768]{0:T(1024)}, u32[]{:S(2)}) copy-start(f32[768]{0:T(1024)} %get-tuple-element.57) | copy-start | bytes 9220
  25.2 2.1 %copy-start.1 = (bf16[17,34,768]{2,0,1:T(8,128)(2,1)}, bf16[17,34,768]{2,0,1:T(8,128)(2,1)S(1)}, u32[]{:S(2)}) copy-start(bf16[17,34,768]{2,0,1:T(8,128)(2,1)S(1)} %get-tuple-element.70) | copy-start | bytes 2663428
  25.2 2.1 %copy-start.3 = (bf16[17,34,768]{2,0,1:T(8,128)(2,1)}, bf16[17,34,768]{2,0,1:T(8,128)(2,1)S(1)}, u32[]{:S(2)}) copy-start(bf16[17,34,768]{2,0,1:T(8,128)(2,1)S(1)} %get-tuple-element.71) | copy-start | bytes 2663428
  37.5 2.5 %copy-start.12 = (bf16[8,8,768]{2,1,0:T(8,128)(2,1)S(1)}, bf16[8,8,768]{2,1,0:T(8,128)(2,1)}, u32[]{:S(2)}) copy-start(bf16[8,8,768]{2,1,0:T(8,128)(2,1)} %shard_map.95) | copy-start | bytes 294916
  52.6 1.8 %copy-start.14 = (bf16[12,64,512]{2,1,0:T(8,128)(2,1)}, bf16[12,64,512]{2,1,0:T(8,128)(2,1)S(1)}, u32[]{:S(2)}) copy-start(bf16[12,64,512]{2,1,0:T(8,128)(2,1)S(1)} %convolution_convert_fusion.5) | copy-start | bytes 2359300
  52.6 1.8 %copy-start.10 = (bf16[64,768]{0,1:T(8,128)(2,1)S(1)}, bf16[64,768]{0,1:T(8,128)(2,1)}, u32[]{:S(2)}) copy-start(bf16[64,768]{0,1:T(8,128)(2,1)} %copy.170) | copy-start | bytes 294916
  62.5 16.3 %copy-start.6 = (bf16[768,768]{1,0:T(8,128)(2,1)S(1)}, bf16[768,768]{1,0:T(8,128)(2,1)}, u32[]{:S(2)}) copy-start(bf16[768,768]{1,0:T(8,128)(2,1)} %param.10) | copy-start | bytes 3538948
  62.5 16.7 %copy-start.7 = (bf16[768,768]{1,0:T(8,128)(2,1)S(1)}, bf16[768,768]{1,0:T(8,128)(2,1)}, u32[]{:S(2)}) copy-start(bf16[768,768]{1,0:T(8,128)(2,1)} %param.11) | copy-start | bytes 3538948
  77.3 2.4 %copy-start.23 = (f32[8,768]{1,0:T(8,128)S(1)}, f32[8,768]{1,0:T(8,128)}, u32[]{:S(2)}) copy-start(f32[8,768]{1,0:T(8,128)} %copy-done.22) | copy-start | bytes 73732
  77.3 2.4 %copy-start.41 = (f32[8]{0:T(128)S(1)}, f32[8]{0:T(128)}, u32[]{:S(2)}) copy-start(f32[8]{0:T(128)} %copy-done.40) | copy-start | bytes 100
  77.3 2.4 %copy-start.43 = (f32[8]{0:T(128)S(1)}, f32[8]{0:T(128)}, u32[]{:S(2)}) copy-start(f32[8]{0:T(128)} %copy-done.42) | copy-start | bytes 100
  81.2 2.3 %copy-start.15 = (bf16[768,768]{1,0:T(8,128)(2,1)S(1)}, bf16[768,768]{1,0:T(8,128)(2,1)}, u32[]{:S(2)}) copy-start(bf16[768,768]{1,0:T(8,128)(2,1)} %convolution_convert_fusion) | copy-start | bytes 3538948
  90.1 5.8 %copy-start.2 = (bf16[17,34,768]{2,0,1:T(8,128)(2,1)S(1)}, bf16[17,34,768]{2,0,1:T(8,128)(2,1)}, u32[]{:S(2)}) copy-start(bf16[17,34,768]{2,0,1:T(8,128)(2,1)} %copy-done.1) | copy-start | bytes 2663428
  90.1 5.8 %copy-start.5 = (bf16[16,32,768]{2,0,1:T(8,128)(2,1)S(1)}, bf16[16,32,768]{2,0,1:T(8,128)(2,1)}, u32[]{:S(2)}) copy-start(bf16[16,32,768]{2,0,1:T(8,128)(2,1)} %copy-done.4) | copy-start | bytes 2359300
  90.1 5.8 %copy-start.19 = (bf16[16,1,768]{2,0,1:T(8,128)(2,1)S(1)}, bf16[16,1,768]{2,0,1:T(8,128)(2,1)}, u32[]{:S(2)}) copy-start(bf16[16,1,768]{2,0,1:T(8,128)(2,1)} %get-tuple-element.102) | copy-start | bytes 73732
  90.1 5.8 %copy-start.21 = (bf16[16,1,768]{2,0,1:T(8,128)(2,1)S(1)}, bf16[16,1,768]{2,0,1:T(8,128)(2,1)}, u32[]{:S(2)}) copy-start(bf16[16,1,768]{2,0,1:T(8,128)(2,1)} %get-tuple-element.103) | copy-start | bytes 73732
  102.7 17.9 %copy-start.13 = (bf16[8,8,768]{2,1,0:T(8,128)(2,1)S(1)}, bf16[8,8,768]{2,1,0:T(8,128)(2,1)}, u32[]{:S(2)}) copy-start(bf16[8,8,768]{2,1,0:T(8,128)(2,1)} %shard_map.95) | copy-start | bytes 294916
  162.6 2.8 %copy-start.26 = (bf16[4,16,768]{2,1,0:T(8,128)(2,1)S(1)}, bf16[4,16,768]{2,1,0:T(8,128)(2,1)}, u32[]{:S(2)}) copy-start(bf16[4,16,768]{2,1,0:T(8,128)(2,1)} %get-tuple-element.17) | copy-start | bytes 294916
  162.6 2.9 %copy-start.25 = (bf16[2,32,768]{2,1,0:T(8,128)(2,1)S(1)}, bf16[2,32,768]{2,1,0:T(8,128)(2,1)}, u32[]{:S(2)}) copy-start(bf16[2,32,768]{2,1,0:T(8,128)(2,1)} %get-tuple-element.18) | copy-start | bytes 294916
  162.6 3.1 %copy-start.8 = (bf16[16,32,768]{2,0,1:T(8,128)(2,1)S(1)}, bf16[16,32,768]{2,0,1:T(8,128)(2,1)}, u32[]{:S(2)}) copy-start(bf16[16,32,768]{2,0,1:T(8,128)(2,1)} %get-tuple-element.63) | copy-start | bytes 2359300
  165.8 1.4 copy-start.11
  165.8 1.4 copy-start.28
  165.8 1.4 copy-start.30
  (14 other events, 16.0 us)

commit v2 on v0

v2 whole, which is shorter than its diff:
```python
from functools import partial

import jax
import jax.numpy as jnp
from jax import lax
from jax.experimental import pallas as pl
from jax.experimental.pallas import tpu as pltpu
from jax.sharding import PartitionSpec as P

HD = 64
POOL = 8
LANES = 128
EDGE = 8

EPSILON = 1e-05
MESH = pl.DeviceIdType.MESH
VMEM = pl.BlockSpec(memory_space=pltpu.VMEM)
DIRECTIONS = ((-1, 0), (1, 0), (0, -1), (0, 1), (-1, -1), (-1, 1), (1, -1), (1, 1))
F32 = jnp.float32
BF16 = jnp.bfloat16


def contract(left, right, at_left, at_right):
    return lax.dot_general(
        left, right, (((at_left,), (at_right,)), ((), ())), preferred_element_type=F32
    )


def split(value):
    high = value.astype(BF16)
    return high, (value - high.astype(F32)).astype(BF16)


def remote(source, target, send, recv, row, col):
    return pltpu.make_async_remote_copy(
        src_ref=source,
        dst_ref=target,
        send_sem=send,
        recv_sem=recv,
        device_id=(row, col),
        device_id_type=MESH,
    )


def block_kernel(rows_n, cols_n, names, *refs):
    r = dict(zip(names, refs, strict=True))
    image, grad_out, taps = r["image"], r["grad_out"], r["taps"]
    pad1, pad2 = r["pad1"], r["pad2"]
    hidden, query, dout = r["hidden"], r["query"], r["dout"]
    attended, grad_query = r["attended"], r["grad_query"]
    height, width, channels = image.shape
    own = (height // POOL) * (width // POOL)
    per_row = width // POOL
    cells_n = cols_n * own
    shard = r["terms"].shape[4]
    row, col = lax.axis_index("row"), lax.axis_index("col")
    chip, core = col // 2, lax.rem(col, 2)
    chips, items = cols_n // 2, cols_n // 4
    half = items // 2
    is_cells = jnp.logical_and(chip >= half, chip < chips - half)
    is_terms = jnp.logical_or(chip < half, chip >= chips - half)

    def row_mate(step):
        return lax.rem(row + step, rows_n)

    def col_mate(step):
        return lax.rem(col + step, cols_n)

    def present(down, right):
        ok = None
        for move, at, count in ((down, row, rows_n), (right, col, cols_n)):
            if move == 0:
                continue
            here = at > 0 if move < 0 else at < count - 1
            ok = here if ok is None else jnp.logical_and(ok, here)
        return ok

    for pad in (pad1, pad2):
        for at in (0, height + 1):
            pad[at] = jnp.zeros_like(pad[at])
    for name in ("edges_in1", "edges_in2"):
        r[name][...] = jnp.zeros_like(r[name])

    barrier = pltpu.get_barrier_semaphore()
    greeted = cols_n + rows_n - 2
    for down, right in DIRECTIONS:
        greeted = greeted + present(down, right).astype(jnp.int32)

        @pl.when(present(down, right))
        def _(down=down, right=right):
            pl.semaphore_signal(barrier, inc=1, device_id=(row + down, col + right), device_id_type=MESH)
    for step in range(1, cols_n):
        pl.semaphore_signal(barrier, inc=1, device_id=(row, col_mate(step)), device_id_type=MESH)
    for step in range(1, rows_n):
        pl.semaphore_signal(barrier, inc=1, device_id=(row_mate(step), col), device_id_type=MESH)

    middle = pl.ds(EDGE, width)
    near, far = pl.ds(EDGE, EDGE), pl.ds(width, EDGE)
    before, after = pl.ds(0, EDGE), pl.ds(EDGE + width, EDGE)

    def edge(number, at):
        pad, out, got = (pad1, r["edges_out1"], r["edges_in1"]) if number == 1 else (pad2, r["edges_out2"], r["edges_in2"])
        down, right = DIRECTIONS[at]
        source = 1 if down < 0 else height
        target = height + 1 if down < 0 else 0
        if down == 0:
            source_ref, target_ref = out.at[0 if right < 0 else 1], got.at[1 if right < 0 else 0]
        elif right == 0:
            source_ref, target_ref = pad.at[source, middle], pad.at[target, middle]
        elif right < 0:
            source_ref, target_ref = pad.at[source, near], pad.at[target, after]
        else:
            source_ref, target_ref = pad.at[source, far], pad.at[target, before]
        return remote(
            source_ref, target_ref, r[f"halo_send{number}"].at[at], r[f"halo_recv{number}"].at[at], row + down, col + right
        )

    def send_halo(number):
        pad, out = (pad1, r["edges_out1"]) if number == 1 else (pad2, r["edges_out2"])
        for at in range(height):
            out[0, at : at + 1] = pad[at + 1, EDGE : EDGE + 1]
            out[1, at : at + 1] = pad[at + 1, EDGE + width - 1 : EDGE + width]
        for at, (down, right) in enumerate(DIRECTIONS):
            @pl.when(present(down, right))
            def _(at=at):
                edge(number, at).start()

    def take_halo(number):
        pad, got = (pad1, r["edges_in1"]) if number == 1 else (pad2, r["edges_in2"])
        for at, (down, right) in enumerate(DIRECTIONS):
            @pl.when(present(-down, -right))
            def _(at=at):
                edge(number, at).wait_recv()

            @pl.when(present(down, right))
            def _(at=at):
                edge(number, at).wait_send()
        for at in range(height):
            pad[at + 1, EDGE - 1 : EDGE] = got[0, at : at + 1]
            pad[at + 1, EDGE + width : EDGE + width + 1] = got[1, at : at + 1]

    @pl.loop(0, height)
    def _(at):
        pad1[at + 1, middle] = image[at].astype(F32)

    pl.semaphore_wait(barrier, greeted)
    send_halo(1)

    tokens = height * width
    chunk = tokens // 2

    @pl.loop(0, 2)
    def _(at):
        rows = pl.ds(pl.multiple_of(at * chunk, chunk), chunk)
        dout[rows] = contract(grad_out[rows], r["w_out"][...], 1, 1).astype(BF16)

    take_halo(1)

    @pl.loop(0, channels // LANES)
    def _(part):
        lanes = pl.ds(pl.multiple_of(part * LANES, LANES), LANES)
        weight = [jnp.broadcast_to(taps[i : i + 1, lanes], (width, LANES)) for i in range(9)]
        for cell_row in range(height // POOL):
            pooled = jnp.zeros((width, LANES), F32)
            for at in range(cell_row * POOL, (cell_row + 1) * POOL):
                total = jnp.zeros((width, LANES), F32)
                for i in range(9):
                    total = total + weight[i] * pad1[at + i // 3, pl.ds(EDGE - 1 + i % 3, width), lanes]
                value = (pad1[at + 1, middle, lanes] + total).astype(BF16)
                hidden[at * width : (at + 1) * width, lanes] = value
                pooled = pooled + value.astype(F32)
            r["pooled"][cell_row * per_row : (cell_row + 1) * per_row, lanes] = (
                pooled.reshape(per_row, POOL, LANES).sum(axis=1) / (POOL * POOL)
            )

    pooled = r["pooled"][...]
    centre = jnp.mean(pooled, axis=-1, keepdims=True)
    spread = jnp.mean(jnp.square(pooled - centre), axis=-1, keepdims=True)
    inverse = lax.rsqrt(spread + EPSILON)
    standard = (pooled - centre) * inverse
    cellbuf = r["cellbuf"]
    cellbuf[col] = standard.astype(BF16).astype(F32)

    def cell(step):
        return remote(
            cellbuf.at[col], cellbuf.at[col], r["cell_send"].at[step - 1], r["cell_recv"].at[step - 1], row, col_mate(step)
        )

    for step in range(1, cols_n):
        cell(step).start()

    @pl.loop(0, 2)
    def _(at):
        rows = pl.ds(pl.multiple_of(at * chunk, chunk), chunk)
        query[rows] = contract(hidden[rows], r["w_query"][...], 1, 0).astype(BF16)

    for step in range(1, cols_n):
        cell(step).wait()
    key_cells = cellbuf[...].reshape(cells_n, channels).astype(BF16)
    r["key_all"][row] = key_cells
    r["keys"][...] = contract(key_cells, r["w_key"][...], 1, 0).astype(BF16)
    r["values"][...] = contract(key_cells, r["w_value"][...], 1, 0).astype(BF16)

    pair_cells = 2 * cells_n
    same_head = (
        lax.broadcasted_iota(jnp.int32, (pair_cells, LANES), 0) // cells_n
        == lax.broadcasted_iota(jnp.int32, (pair_cells, LANES), 1) // HD
    )
    cell_ones = (
        lax.broadcasted_iota(jnp.int32, (pair_cells, pair_cells), 0) // cells_n
        == lax.broadcasted_iota(jnp.int32, (pair_cells, pair_cells), 1) // cells_n
    ).astype(F32).astype(BF16)
    lane_ones = (
        lax.broadcasted_iota(jnp.int32, (LANES, pair_cells), 0) // HD
        == lax.broadcasted_iota(jnp.int32, (LANES, pair_cells), 1) // cells_n
    ).astype(F32).astype(BF16)
    first_head = lax.broadcasted_iota(jnp.int32, (cells_n, LANES), 1) < HD
    scale = HD ** (-0.5)

    def summed(value, ones):
        high, low = split(value)
        return contract(high, ones, 1, 0) + contract(low, ones, 1, 0)

    @pl.loop(0, channels // LANES)
    def _(part):
        lanes = pl.ds(pl.multiple_of(part * LANES, LANES), LANES)

        def both(ref):
            value = ref[:, lanes].astype(F32)
            twice = jnp.concatenate([value, value], axis=0)
            return jnp.where(same_head, twice, 0.0).astype(BF16)

        key_pair, value_pair = both(r["keys"]), both(r["values"])
        queries, douts = query[:, lanes], dout[:, lanes]
        expons = jnp.exp(contract(queries, key_pair, 1, 1) * scale)
        probabilities = expons / summed(expons, cell_ones)
        weights = probabilities.astype(BF16)
        got = contract(weights, value_pair, 1, 0).astype(BF16)
        attended[:, lanes] = got
        grad_probs = contract(douts, value_pair, 1, 1)
        deltas = summed(douts.astype(F32) * got.astype(F32), lane_ones)
        grad_scores = (probabilities * (grad_probs - deltas) * scale).astype(BF16)
        grad_query[:, lanes] = contract(grad_scores, key_pair, 1, 0).astype(BF16)
        grad_key = contract(grad_scores, queries, 0, 0)
        grad_value = contract(weights, douts, 0, 0)
        grad_key = jnp.where(first_head, grad_key[:cells_n], grad_key[cells_n:])
        grad_value = jnp.where(first_head, grad_value[:cells_n], grad_value[cells_n:])
        for owner in range(cols_n):
            rows = slice(owner * own, (owner + 1) * own)
            r["blocks"][owner, :, lanes] = jnp.concatenate([grad_key[rows], grad_value[rows]], axis=0).astype(BF16)

    def block(step):
        owner = col_mate(step)
        return remote(
            r["blocks"].at[owner], r["blocks_in"].at[step - 1], r["block_send"].at[step - 1], r["block_recv"].at[step - 1], row, owner
        )

    for step in range(1, cols_n):
        block(step).start()

    terms, landed1, held1 = r["terms"], r["landed1"], r["held1"]
    landed2, held2, landed3, summed_all = r["landed2"], r["held2"], r["landed3"], r["summed_all"]

    def first(item):
        return remote(
            terms.at[1 - core, item], landed1.at[item], r["send1"].at[item], r["recv1"].at[item], row, 2 * chip + 1 - core
        )

    def second(item, step):
        return remote(
            held1.at[item, row_mate(step)], landed2.at[item, step - 1], r["send2"].at[item, step - 1],
            r["recv2"].at[item, step - 1], row_mate(step), col,
        )

    def owner_of(item):
        return item if item < half else chips - items + item

    def third(item):
        return remote(
            held2.at[item], landed3.at[chip], r["send3"].at[item], r["recv3"].at[chip], row, 2 * owner_of(item) + core
        )

    def fourth(step):
        return remote(
            summed_all.at[row], summed_all.at[row], r["send4"].at[step - 1], r["recv4"].at[step - 1], row_mate(step), col
        )

    for left, right, begin in ((hidden, grad_query, 0), (attended, grad_out, half)):
        for item in range(half):
            for side in range(2):
                at = (2 * item + side) * shard
                term = contract(left[...], right[:, at : at + shard], 0, 0).astype(BF16)
                terms[side, begin + item] = term.reshape(terms.shape[2:])
            first(begin + item).start()

    @pl.loop(0, 2)
    def _(at):
        rows = pl.ds(pl.multiple_of(at * chunk, chunk), chunk)
        value = contract(grad_query[rows], r["w_query"][...], 1, 1) + grad_out[rows].astype(F32)
        pad2[pl.ds(1 + at * (height // 2), height // 2), middle] = value.reshape(height // 2, width, channels)

    totals = r["blocks"][col].astype(F32)
    for step in range(1, cols_n):
        block(step).wait()
        totals = totals + r["blocks_in"][step - 1].astype(F32)
    high, low = split(totals)
    tot_all = r["tot_all"]
    tot_all[col] = high

    def tot(step):
        return remote(
            tot_all.at[col], tot_all.at[col], r["tot_send"].at[step - 1], r["tot_recv"].at[step - 1], row, col_mate(step)
        )

    for step in range(1, cols_n):
        tot(step).start()

    both_parts = jnp.concatenate([high, low], axis=0)
    by_key = contract(both_parts, r["w_key"][...], 1, 1)
    by_value = contract(both_parts, r["w_value"][...], 1, 1)
    grad_normed = by_key[:own] + by_key[2 * own : 3 * own] + by_value[own : 2 * own] + by_value[3 * own :]
    grad_pooled = (
        grad_normed
        - jnp.mean(grad_normed, axis=-1, keepdims=True)
        - standard * jnp.mean(grad_normed * standard, axis=-1, keepdims=True)
    ) * inverse
    grad_pooled = grad_pooled / (POOL * POOL)
    for cell_row in range(height // POOL):
        rows = grad_pooled[cell_row * per_row : (cell_row + 1) * per_row]
        over = jnp.broadcast_to(rows[:, None, :], (per_row, POOL, channels)).reshape(width, channels)
        r["over"][cell_row] = over

    @pl.loop(0, height)
    def _(at):
        pad2[at + 1, middle] = pad2[at + 1, middle] + r["over"][at // POOL]

    send_halo(2)

    for item in range(items):
        first(item).wait_recv()
        for step in range(1, rows_n + 1):
            there = row_mate(step)
            held1[item, there] = (
                terms[core, item, there].astype(F32) + landed1[item, there].astype(F32)
            ).astype(BF16)
            if step < rows_n:
                second(item, step).start()

    r["tap_terms"][...] = jnp.zeros_like(r["tap_terms"])

    @pl.loop(0, channels // LANES)
    def _(part):
        lanes = pl.ds(pl.multiple_of(part * LANES, LANES), LANES)
        sums = [jnp.zeros((8, LANES), F32) for _ in range(9)]
        for at in range(height):
            value = pad2[at + 1, middle, lanes]
            for i in range(9):
                product = value * pad1[at + i // 3, pl.ds(EDGE - 1 + i % 3, width), lanes]
                sums[i] = sums[i] + product.reshape(width // 8, 8, LANES).sum(axis=0)
        for i in range(9):
            r["tap_terms"][i : i + 1, lanes] = sums[i].sum(axis=0, keepdims=True)

    tap_out, tap_in, tap_out2, tap_in2 = r["tap_out"], r["tap_in"], r["tap_out2"], r["tap_in2"]
    tap_out[...] = r["tap_terms"][...].astype(BF16)

    def tap_first(step):
        return remote(tap_out, tap_in.at[step - 1], r["tap_send1"].at[step - 1], r["tap_recv1"].at[step - 1], row_mate(step), col)

    def tap_second(step):
        return remote(tap_out2, tap_in2.at[step - 1], r["tap_send2"].at[step - 1], r["tap_recv2"].at[step - 1], row, col_mate(step))

    for step in range(1, rows_n):
        tap_first(step).start()

    for item in range(items):
        total = held1[item, row].astype(F32)
        for step in range(1, rows_n):
            second(item, step).wait_recv()
            total = total + landed2[item, step - 1].astype(F32)
        held2[item] = total.astype(BF16)

        @pl.when(chip != owner_of(item))
        def _(item=item):
            third(item).start()

    for step in range(1, cols_n):
        tot(step).wait()
    is_key = col < 2 * items
    sides = []
    for at in range(cols_n):
        value = tot_all[at].astype(F32)
        sides.append(jnp.where(is_key, value[:own], value[own:]))
    r["side_all"][row] = jnp.concatenate(sides, axis=0).astype(BF16)

    def pass_on(name, step):
        return remote(
            r[name].at[row], r[name].at[row], r[name + "_send"].at[step - 1], r[name + "_recv"].at[step - 1], row_mate(step), col
        )

    @pl.when(is_cells)
    def _():
        for name in ("key_all", "side_all"):
            for step in range(1, rows_n):
                pass_on(name, step).start()

    tap_total = tap_out[...].astype(F32)
    for step in range(1, rows_n):
        tap_first(step).wait()
        tap_total = tap_total + tap_in[step - 1].astype(F32)
    tap_out2[...] = tap_total.astype(BF16)
    for step in range(1, cols_n):
        tap_second(step).start()

    take_halo(2)

    @pl.loop(0, channels // LANES)
    def _(part):
        lanes = pl.ds(pl.multiple_of(part * LANES, LANES), LANES)
        weight = [jnp.broadcast_to(taps[i : i + 1, lanes], (width, LANES)) for i in range(9)]
        for at in range(height):
            total = pad2[at + 1, middle, lanes]
            for i in range(9):
                total = total + weight[i] * pad2[at + 2 - i // 3, pl.ds(EDGE + 1 - i % 3, width), lanes]
            r["grad_image"][at, :, lanes] = total.astype(BF16)

    @pl.when(is_terms)
    def _():
        mine = lax.rem(chip, chips - items)
        total = held2[mine].astype(F32)
        for step in range(1, chips):
            source = lax.rem(chip + step, chips)
            remote(
                held2.at[0], landed3.at[source], r["send3"].at[0], r["recv3"].at[source], row, 2 * source + core
            ).wait_recv()
            total = total + landed3[source].astype(F32)
        summed_all[row] = total.astype(BF16)
        for step in range(1, rows_n):
            fourth(step).start()

    tap_total = tap_out2[...].astype(F32)
    for step in range(1, cols_n):
        tap_second(step).wait()
        tap_total = tap_total + tap_in2[step - 1].astype(F32)
    r["tap_sum"][...] = tap_total

    for item in range(items):
        first(item).wait_send()
        for step in range(1, rows_n):
            second(item, step).wait_send()

        @pl.when(chip != owner_of(item))
        def _(item=item):
            third(item).wait_send()

    @pl.when(is_terms)
    def _():
        for step in range(1, rows_n):
            fourth(step).wait()

    @pl.when(is_cells)
    def _():
        for name in ("key_all", "side_all"):
            for step in range(1, rows_n):
                pass_on(name, step).wait()


def on_device(image, conv_taps, w_query, w_key, w_value, w_out, grad_out):
    rows_n, cols_n = lax.axis_size("row"), lax.axis_size("col")
    height, width, channels = image.shape
    tokens = height * width
    own = (height // POOL) * (width // POOL)
    cells_n = cols_n * own
    chips, items = cols_n // 2, cols_n // 4
    shard = 4 * channels // cols_n
    high = channels // rows_n
    operands = dict(
        image=image, grad_out=grad_out.reshape(tokens, channels), taps=conv_taps,
        w_query=w_query, w_key=w_key, w_value=w_value, w_out=w_out,
    )
    shapes = dict(
        grad_image=(image.shape, BF16),
        summed_all=((rows_n, high, shard), BF16),
        key_all=((rows_n, cells_n, channels), BF16),
        side_all=((rows_n, cells_n, channels), BF16),
        tap_sum=((16, channels), F32),
    )
    scratch = dict(
        pad1=((height + 2, width + 2 * EDGE, channels), F32),
        pad2=((height + 2, width + 2 * EDGE, channels), F32),
        edges_out1=((2, height, channels), F32), edges_in1=((2, height, channels), F32),
        edges_out2=((2, height, channels), F32), edges_in2=((2, height, channels), F32),
        hidden=((tokens, channels), BF16), query=((tokens, channels), BF16), dout=((tokens, channels), BF16),
        attended=((tokens, channels), BF16), grad_query=((tokens, channels), BF16),
        pooled=((own, channels), F32), over=((height // POOL, width, channels), F32),
        cellbuf=((cols_n, own, channels), F32),
        keys=((cells_n, channels), BF16), values=((cells_n, channels), BF16),
        blocks=((cols_n, 2 * own, channels), BF16), blocks_in=((cols_n - 1, 2 * own, channels), BF16),
        tot_all=((cols_n, 2 * own, channels), BF16),
        terms=((2, items, rows_n, high, shard), BF16),
        landed1=((items, rows_n, high, shard), BF16), held1=((items, rows_n, high, shard), BF16),
        landed2=((items, rows_n - 1, high, shard), BF16), held2=((items, high, shard), BF16),
        landed3=((chips, high, shard), BF16),
        tap_terms=((16, channels), F32),
        tap_out=((16, channels), BF16), tap_in=((rows_n - 1, 16, channels), BF16),
        tap_out2=((16, channels), BF16), tap_in2=((cols_n - 1, 16, channels), BF16),
    )
    sems = dict(
        halo_send1=(8,), halo_recv1=(8,), halo_send2=(8,), halo_recv2=(8,),
        cell_send=(cols_n - 1,), cell_recv=(cols_n - 1,),
        block_send=(cols_n - 1,), block_recv=(cols_n - 1,),
        tot_send=(cols_n - 1,), tot_recv=(cols_n - 1,),
        send1=(items,), recv1=(items,), send2=(items, rows_n - 1), recv2=(items, rows_n - 1),
        send3=(items,), recv3=(chips,), send4=(rows_n - 1,), recv4=(rows_n - 1,),
        tap_send1=(rows_n - 1,), tap_recv1=(rows_n - 1,),
        tap_send2=(cols_n - 1,), tap_recv2=(cols_n - 1,),
        key_all_send=(rows_n - 1,), key_all_recv=(rows_n - 1,),
        side_all_send=(rows_n - 1,), side_all_recv=(rows_n - 1,),
    )
    names = list(operands) + list(shapes) + list(scratch) + list(sems)
    grad_image, summed_all, key_all, side_all, tap_sum = pl.pallas_call(
        partial(block_kernel, rows_n, cols_n, names),
        out_shape=[jax.ShapeDtypeStruct(*spec) for spec in shapes.values()],
        in_specs=[VMEM] * len(operands),
        out_specs=[VMEM] * len(shapes),
        scratch_shapes=[pltpu.VMEM(*spec) for spec in scratch.values()]
        + [pltpu.SemaphoreType.DMA(spec) for spec in sems.values()],
        compiler_params=pltpu.CompilerParams(
            collective_id=0, has_side_effects=True, vmem_limit_bytes=60 * 2**20
        ),
    )(*operands.values())
    quarter = cols_n // 4
    col = lax.axis_index("col")
    mine = lax.dynamic_slice_in_dim(
        side_all.reshape(-1, channels), lax.rem(col, quarter) * shard, shard, axis=1
    )
    from_cells = contract(key_all.reshape(-1, channels), mine, 0, 0)
    is_cells = jnp.logical_and(col >= quarter, col < cols_n - quarter)
    grad_weights = jnp.where(is_cells, from_cells, summed_all.reshape(channels, shard).astype(F32))
    grad_conv = lax.dynamic_slice_in_dim(
        tap_sum[:9], col * (channels // cols_n), channels // cols_n, axis=1
    )
    return (grad_image, grad_weights, grad_conv)


def solution(mesh):
    return jax.shard_map(
        on_device,
        mesh=mesh,
        in_specs=(P("row", "col", None), P(), P(), P(), P(), P(), P("row", "col", None)),
        out_specs=(P("row", "col", None), P(None, "col"), P(None, "col")),
        check_vma=False,
    )
```

time: 295 us -> 85.9 us (0.29)
  the two profiles are of different devices: /device:TPU:0 before, /device:TPU:24 now
where the time goes in v2:
time: 85.9 us; the launch traced here: 85.7 us
  Pallas kernels  80 us (93%)
  matrix products  2.76 us (3%)
  local copies, waits for them, and re-layouts  2.27 us (3%)
    pallas_call x1, Pallas kernels, on_device(): pl.pallas_call(partial(block_kernel, rows_n, cols_n, names), out_shape=[j...  80 us
    dot_general x1, matrix products, contract(): lax.dot_general(left, right, (((at_left,), (at_right,)), ((), ())), prefe...  2.76 us

profile of v2, /device:TPU:24, one launch (start us, length us, event | category | flops | bytes accessed | tf_op | source)
XLA Modules:
  0.0 85.7 jit_solution(1700862525724673241)
XLA Ops:
  0.6 80.0 %shard_map.94 = (bf16[16,32,768]{2,1,0:T(8,128)(2,1)}, bf16[4,192,384]{2,1,0:T(8,128)(2,1)}, bf16[4,64,768]{2,1,0:T(8,128)(2,1)}, bf16[4,64,768]{2,1,0:T(8,128)(2,1)}, f32[16,768]{1,0:T(8,128)}) custom-call(bf16[16,32,768]{2,1,0:T(8,128)(2,1)} %refs_0_.1, bf16[512,768]{1,0:T(8,128)(2,1)} %bitcast.7, f32[9,768]{1,0:T(8,128)} %refs_2_.1, ...), custom_call_target="tpu_custom_call" | custom-call | tf_op jit(solution)/shard_map/pallas_call | solution.py:520
  80.6 0.0 copy-start
  80.6 2.8 %convolution_select_fusion = f32[768,384]{1,0:T(8,128)} fusion(bf16[256,768]{1,0:T(8,128)(2,1)} %bitcast.9, bf16[768,384]{1,0:T(8,128)(2,1)} %bitcast.8, pred[]{:T(512)S(6)} %and.5, bf16[256,768]{1,0:T(8,128)(2,1)} %bitcast.10, s32[]{:T(128)S(6)} %select_n.15), kind=kOutput, calls=%fused_computation | convolution fusion | flops 151584768 | bytes 2359301 | tf_op jit(solution)/shard_map/dot_general | solution.py:24
  83.4 1.4 %constant_dynamic-slice_fusion = f32[9,96]{1,0:T(8,128)} fusion(f32[9,768]{1,0:T(8,128)} %bitcast.11, s32[]{:T(128)S(6)} %select_n.17), kind=kLoop, calls=%fused_computation.2 | loop fusion | bytes 6916 | tf_op jit(solution)/shard_map/dynamic_slice | solution.py:539
  84.8 0.0 copy-done
  84.8 0.9 %copy.11 = bf16[16,32,768]{2,1,0:T(8,128)(2,1)} copy(bf16[16,32,768]{2,1,0:T(8,128)(2,1)S(1)} %copy-done) | data formatting | bytes 1572864
Async XLA Ops:
  80.6 4.2 %copy-start = (bf16[16,32,768]{2,1,0:T(8,128)(2,1)S(1)}, bf16[16,32,768]{2,1,0:T(8,128)(2,1)}, u32[]{:S(2)}) copy-start(bf16[16,32,768]{2,1,0:T(8,128)(2,1)} %get-tuple-element.16) | copy-start | bytes 2359300

commit v3 on v2

--- a/solution.py
+++ b/solution.py
@@ -266,24 +266,71 @@
             terms.at[1 - core, item], landed1.at[item], r["send1"].at[item], r["recv1"].at[item], row, 2 * chip + 1 - core
         )
 
-    def second(item, step):
-        return remote(
-            held1.at[item, row_mate(step)], landed2.at[item, step - 1], r["send2"].at[item, step - 1],
-            r["recv2"].at[item, step - 1], row_mate(step), col,
+    deep = terms.shape[3] // 2
+    part_of = [pl.ds(sub * deep, deep) for sub in range(2)]
+
+    def second(item, step, sub):
+        return remote(
+            held1.at[item, row_mate(step), part_of[sub]], landed2.at[item, step - 1, part_of[sub]],
+            r["send2"].at[item, step - 1, sub], r["recv2"].at[item, step - 1, sub], row_mate(step), col,
         )
 
     def owner_of(item):
         return item if item < half else chips - items + item
 
-    def third(item):
-        return remote(
-            held2.at[item], landed3.at[chip], r["send3"].at[item], r["recv3"].at[chip], row, 2 * owner_of(item) + core
-        )
-
-    def fourth(step):
-        return remote(
-            summed_all.at[row], summed_all.at[row], r["send4"].at[step - 1], r["recv4"].at[step - 1], row_mate(step), col
-        )
+    def third(item, sub):
+        return remote(
+            held2.at[item, part_of[sub]], landed3.at[chip, part_of[sub]], r["send3"].at[item, sub],
+            r["recv3"].at[chip, sub], row, 2 * owner_of(item) + core,
+        )
+
+    def fourth(step, sub):
+        return remote(
+            summed_all.at[row, part_of[sub]], summed_all.at[row, part_of[sub]], r["send4"].at[step - 1, sub],
+            r["recv4"].at[step - 1, sub], row_mate(step), col,
+        )
+
+    def start_second():
+        for sub in range(2):
+            for item in range(items):
+                if sub == 0:
+                    first(item).wait_recv()
+                for step in range(1, rows_n + 1):
+                    there = row_mate(step)
+                    held1[item, there, part_of[sub]] = (
+                        terms[core, item, there, part_of[sub]].astype(F32)
+                        + landed1[item, there, part_of[sub]].astype(F32)
+                    ).astype(BF16)
+                    if step < rows_n:
+                        second(item, step, sub).start()
+
+    def start_third(sub):
+        for item in range(items):
+            total = held1[item, row, part_of[sub]].astype(F32)
+            for step in range(1, rows_n):
+                second(item, step, sub).wait_recv()
+                total = total + landed2[item, step - 1, part_of[sub]].astype(F32)
+            held2[item, part_of[sub]] = total.astype(BF16)
+
+            @pl.when(chip != owner_of(item))
+            def _(item=item):
+                third(item, sub).start()
+
+    def start_fourth(sub):
+        @pl.when(is_terms)
+        def _():
+            mine = lax.rem(chip, chips - items)
+            total = held2[mine, part_of[sub]].astype(F32)
+            for step in range(1, chips):
+                source = lax.rem(chip + step, chips)
+                remote(
+                    held2.at[0, part_of[sub]], landed3.at[source, part_of[sub]], r["send3"].at[0, sub],
+                    r["recv3"].at[source, sub], row, 2 * source + core,
+                ).wait_recv()
+                total = total + landed3[source, part_of[sub]].astype(F32)
+            summed_all[row, part_of[sub]] = total.astype(BF16)
+            for step in range(1, rows_n):
+                fourth(step, sub).start()
 
     for left, right, begin in ((hidden, grad_query, 0), (attended, grad_out, half)):
         for item in range(half):
@@ -298,6 +345,8 @@
         rows = pl.ds(pl.multiple_of(at * chunk, chunk), chunk)
         value = contract(grad_query[rows], r["w_query"][...], 1, 1) + grad_out[rows].astype(F32)
         pad2[pl.ds(1 + at * (height // 2), height // 2), middle] = value.reshape(height // 2, width, channels)
+
+    start_second()
 
     totals = r["blocks"][col].astype(F32)
     for step in range(1, cols_n):
@@ -336,16 +385,6 @@
 
     send_halo(2)
 
-    for item in range(items):
-        first(item).wait_recv()
-        for step in range(1, rows_n + 1):
-            there = row_mate(step)
-            held1[item, there] = (
-                terms[core, item, there].astype(F32) + landed1[item, there].astype(F32)
-            ).astype(BF16)
-            if step < rows_n:
-                second(item, step).start()
-
     r["tap_terms"][...] = jnp.zeros_like(r["tap_terms"])
 
     @pl.loop(0, channels // LANES)
@@ -372,16 +411,7 @@
     for step in range(1, rows_n):
         tap_first(step).start()
 
-    for item in range(items):
-        total = held1[item, row].astype(F32)
-        for step in range(1, rows_n):
-            second(item, step).wait_recv()
-            total = total + landed2[item, step - 1].astype(F32)
-        held2[item] = total.astype(BF16)
-
-        @pl.when(chip != owner_of(item))
-        def _(item=item):
-            third(item).start()
+    start_third(0)
 
     for step in range(1, cols_n):
         tot(step).wait()
@@ -411,6 +441,7 @@
     for step in range(1, cols_n):
         tap_second(step).start()
 
+    start_third(1)
     take_halo(2)
 
     @pl.loop(0, channels // LANES)
@@ -423,19 +454,8 @@
                 total = total + weight[i] * pad2[at + 2 - i // 3, pl.ds(EDGE + 1 - i % 3, width), lanes]
             r["grad_image"][at, :, lanes] = total.astype(BF16)
 
-    @pl.when(is_terms)
-    def _():
-        mine = lax.rem(chip, chips - items)
-        total = held2[mine].astype(F32)
-        for step in range(1, chips):
-            source = lax.rem(chip + step, chips)
-            remote(
-                held2.at[0], landed3.at[source], r["send3"].at[0], r["recv3"].at[source], row, 2 * source + core
-            ).wait_recv()
-            total = total + landed3[source].astype(F32)
-        summed_all[row] = total.astype(BF16)
-        for step in range(1, rows_n):
-            fourth(step).start()
+    start_fourth(0)
+    start_fourth(1)
 
     tap_total = tap_out2[...].astype(F32)
     for step in range(1, cols_n):
@@ -446,16 +466,19 @@
     for item in range(items):
         first(item).wait_send()
         for step in range(1, rows_n):
-            second(item, step).wait_send()
+            for sub in range(2):
+                second(item, step, sub).wait_send()
 
         @pl.when(chip != owner_of(item))
         def _(item=item):
-            third(item).wait_send()
+            for sub in range(2):
+                third(item, sub).wait_send()
 
     @pl.when(is_terms)
     def _():
         for step in range(1, rows_n):
-            fourth(step).wait()
+            for sub in range(2):
+                fourth(step, sub).wait()
 
     @pl.when(is_cells)
     def _():
@@ -509,8 +532,8 @@
         cell_send=(cols_n - 1,), cell_recv=(cols_n - 1,),
         block_send=(cols_n - 1,), block_recv=(cols_n - 1,),
         tot_send=(cols_n - 1,), tot_recv=(cols_n - 1,),
-        send1=(items,), recv1=(items,), send2=(items, rows_n - 1), recv2=(items, rows_n - 1),
-        send3=(items,), recv3=(chips,), send4=(rows_n - 1,), recv4=(rows_n - 1,),
+        send1=(items,), recv1=(items,), send2=(items, rows_n - 1, 2), recv2=(items, rows_n - 1, 2),
+        send3=(items, 2), recv3=(chips, 2), send4=(rows_n - 1, 2), recv4=(rows_n - 1, 2),
         tap_send1=(rows_n - 1,), tap_recv1=(rows_n - 1,),
         tap_send2=(cols_n - 1,), tap_recv2=(cols_n - 1,),
         key_all_send=(rows_n - 1,), key_all_recv=(rows_n - 1,),

time: 85.9 us -> 78.7 us (0.916)
  the two profiles are of different devices: /device:TPU:24 before, /device:TPU:0 now
where the time goes in v3:
time: 78.7 us; the launch traced here: 78.5 us
  Pallas kernels  72.8 us (93%)
  matrix products  2.76 us (4%)
  local copies, waits for them, and re-layouts  2.27 us (3%)
    pallas_call x1, Pallas kernels, on_device(): pl.pallas_call(partial(block_kernel, rows_n, cols_n, names), out_shape=[j...  72.8 us
    dot_general x1, matrix products, contract(): lax.dot_general(left, right, (((at_left,), (at_right,)), ((), ())), prefe...  2.76 us

profile of v3, /device:TPU:0, one launch (start us, length us, event | category | flops | bytes accessed | tf_op | source)
XLA Modules:
  0.0 78.5 jit_solution(7200298999299747835)
XLA Ops:
  0.6 72.8 %shard_map.94 = (bf16[16,32,768]{2,1,0:T(8,128)(2,1)}, bf16[4,192,384]{2,1,0:T(8,128)(2,1)}, bf16[4,64,768]{2,1,0:T(8,128)(2,1)}, bf16[4,64,768]{2,1,0:T(8,128)(2,1)}, f32[16,768]{1,0:T(8,128)}) custom-call(bf16[16,32,768]{2,1,0:T(8,128)(2,1)} %refs_0_.1, bf16[512,768]{1,0:T(8,128)(2,1)} %bitcast.7, f32[9,768]{1,0:T(8,128)} %refs_2_.1, ...), custom_call_target="tpu_custom_call" | custom-call | tf_op jit(solution)/shard_map/pallas_call | solution.py:543
  73.5 0.0 copy-start
  73.5 2.8 %convolution_select_fusion = f32[768,384]{1,0:T(8,128)} fusion(bf16[256,768]{1,0:T(8,128)(2,1)} %bitcast.9, bf16[768,384]{1,0:T(8,128)(2,1)} %bitcast.8, pred[]{:T(512)S(6)} %and.5, bf16[256,768]{1,0:T(8,128)(2,1)} %bitcast.10, s32[]{:T(128)S(6)} %select_n.15), kind=kOutput, calls=%fused_computation | convolution fusion | flops 151584768 | bytes 2359301 | tf_op jit(solution)/shard_map/dot_general | solution.py:24
  76.3 1.4 %constant_dynamic-slice_fusion = f32[9,96]{1,0:T(8,128)} fusion(f32[9,768]{1,0:T(8,128)} %bitcast.11, s32[]{:T(128)S(6)} %select_n.17), kind=kLoop, calls=%fused_computation.2 | loop fusion | bytes 6916 | tf_op jit(solution)/shard_map/dynamic_slice | solution.py:562
  77.7 0.0 copy-done
  77.7 0.9 %copy.11 = bf16[16,32,768]{2,1,0:T(8,128)(2,1)} copy(bf16[16,32,768]{2,1,0:T(8,128)(2,1)S(1)} %copy-done) | data formatting | bytes 1572864
Async XLA Ops:
  73.5 4.2 %copy-start = (bf16[16,32,768]{2,1,0:T(8,128)(2,1)S(1)}, bf16[16,32,768]{2,1,0:T(8,128)(2,1)}, u32[]{:S(2)}) copy-start(bf16[16,32,768]{2,1,0:T(8,128)(2,1)} %get-tuple-element.16) | copy-start | bytes 2359300

commit v4 on v3

--- a/solution.py
+++ b/solution.py
@@ -75,10 +75,9 @@
             ok = here if ok is None else jnp.logical_and(ok, here)
         return ok
 
-    for pad in (pad1, pad2):
-        for at in (0, height + 1):
-            pad[at] = jnp.zeros_like(pad[at])
-    for name in ("edges_in1", "edges_in2"):
+    for at in (0, height + 1):
+        pad2[at] = jnp.zeros_like(pad2[at])
+    for name in ("edges_in1", "edges_in2", "rows_in1", "corners_in1"):
         r[name][...] = jnp.zeros_like(r[name])
 
     barrier = pltpu.get_barrier_semaphore()
@@ -105,6 +104,11 @@
         target = height + 1 if down < 0 else 0
         if down == 0:
             source_ref, target_ref = out.at[0 if right < 0 else 1], got.at[1 if right < 0 else 0]
+        elif number == 1 and right == 0:
+            source_ref, target_ref = image.at[source - 1], r["rows_in1"].at[1 if down < 0 else 0]
+        elif number == 1:
+            source_ref = image.at[source - 1, pl.ds(0 if right < 0 else width - 2 * EDGE, 2 * EDGE)]
+            target_ref = r["corners_in1"].at[(2 if down < 0 else 0) + (1 if right < 0 else 0)]
         elif right == 0:
             source_ref, target_ref = pad.at[source, middle], pad.at[target, middle]
         elif right < 0:
@@ -118,16 +122,24 @@
     def send_halo(number):
         pad, out = (pad1, r["edges_out1"]) if number == 1 else (pad2, r["edges_out2"])
         for at in range(height):
-            out[0, at : at + 1] = pad[at + 1, EDGE : EDGE + 1]
-            out[1, at : at + 1] = pad[at + 1, EDGE + width - 1 : EDGE + width]
+            if number == 1:
+                out[0, at : at + 1] = image[at, : 2 * EDGE].astype(F32)[:1]
+                out[1, at : at + 1] = image[at, width - 2 * EDGE :].astype(F32)[2 * EDGE - 1 :]
+            else:
+                out[0, at : at + 1] = pad[at + 1, EDGE : EDGE + 1]
+                out[1, at : at + 1] = pad[at + 1, EDGE + width - 1 : EDGE + width]
+        if number == 1:
+            pl.semaphore_wait(barrier, greeted)
         for at, (down, right) in enumerate(DIRECTIONS):
             @pl.when(present(down, right))
             def _(at=at):
                 edge(number, at).start()
 
-    def take_halo(number):
-        pad, got = (pad1, r["edges_in1"]) if number == 1 else (pad2, r["edges_in2"])
+    def wait_edges(number, wanted):
         for at, (down, right) in enumerate(DIRECTIONS):
+            if (down == 0) not in wanted:
+                continue
+
             @pl.when(present(-down, -right))
             def _(at=at):
                 edge(number, at).wait_recv()
@@ -135,16 +147,18 @@
             @pl.when(present(down, right))
             def _(at=at):
                 edge(number, at).wait_send()
+
+    def take_cols(number):
+        pad, got = (pad1, r["edges_in1"]) if number == 1 else (pad2, r["edges_in2"])
         for at in range(height):
             pad[at + 1, EDGE - 1 : EDGE] = got[0, at : at + 1]
             pad[at + 1, EDGE + width : EDGE + width + 1] = got[1, at : at + 1]
 
+    send_halo(1)
+
     @pl.loop(0, height)
     def _(at):
         pad1[at + 1, middle] = image[at].astype(F32)
-
-    pl.semaphore_wait(barrier, greeted)
-    send_halo(1)
 
     tokens = height * width
     chunk = tokens // 2
@@ -154,24 +168,38 @@
         rows = pl.ds(pl.multiple_of(at * chunk, chunk), chunk)
         dout[rows] = contract(grad_out[rows], r["w_out"][...], 1, 1).astype(BF16)
 
-    take_halo(1)
-
-    @pl.loop(0, channels // LANES)
-    def _(part):
-        lanes = pl.ds(pl.multiple_of(part * LANES, LANES), LANES)
-        weight = [jnp.broadcast_to(taps[i : i + 1, lanes], (width, LANES)) for i in range(9)]
-        for cell_row in range(height // POOL):
-            pooled = jnp.zeros((width, LANES), F32)
-            for at in range(cell_row * POOL, (cell_row + 1) * POOL):
-                total = jnp.zeros((width, LANES), F32)
-                for i in range(9):
-                    total = total + weight[i] * pad1[at + i // 3, pl.ds(EDGE - 1 + i % 3, width), lanes]
-                value = (pad1[at + 1, middle, lanes] + total).astype(BF16)
-                hidden[at * width : (at + 1) * width, lanes] = value
-                pooled = pooled + value.astype(F32)
-            r["pooled"][cell_row * per_row : (cell_row + 1) * per_row, lanes] = (
-                pooled.reshape(per_row, POOL, LANES).sum(axis=1) / (POOL * POOL)
-            )
+    def mix(wanted, begin):
+        @pl.loop(0, channels // LANES)
+        def _(part):
+            lanes = pl.ds(pl.multiple_of(part * LANES, LANES), LANES)
+            weight = [jnp.broadcast_to(taps[i : i + 1, lanes], (width, LANES)) for i in range(9)]
+            for cell_row in range(height // POOL):
+                pooled = jnp.zeros((width, LANES), F32)
+                some = False
+                for at in range(cell_row * POOL, (cell_row + 1) * POOL):
+                    if at not in wanted:
+                        continue
+                    some = True
+                    total = jnp.zeros((width, LANES), F32)
+                    for i in range(9):
+                        total = total + weight[i] * pad1[at + i // 3, pl.ds(EDGE - 1 + i % 3, width), lanes]
+                    value = (pad1[at + 1, middle, lanes] + total).astype(BF16)
+                    hidden[at * width : (at + 1) * width, lanes] = value
+                    pooled = pooled + value.astype(F32)
+                if some:
+                    where = slice(cell_row * per_row, (cell_row + 1) * per_row)
+                    sums = pooled.reshape(per_row, POOL, LANES).sum(axis=1) / (POOL * POOL)
+                    r["pooled"][where, lanes] = sums if begin else r["pooled"][where, lanes] + sums
+
+    wait_edges(1, (True,))
+    take_cols(1)
+    mix(range(1, height - 1), True)
+    wait_edges(1, (False,))
+    for at, side in ((0, 0), (height + 1, 1)):
+        pad1[at, middle] = r["rows_in1"][side].astype(F32)
+        pad1[at, EDGE - 1 : EDGE] = r["corners_in1"][2 * side].astype(F32)[2 * EDGE - 1 :]
+        pad1[at, EDGE + width : EDGE + width + 1] = r["corners_in1"][2 * side + 1].astype(F32)[:1]
+    mix((0, height - 1), False)
 
     pooled = r["pooled"][...]
     centre = jnp.mean(pooled, axis=-1, keepdims=True)
@@ -179,7 +207,7 @@
     inverse = lax.rsqrt(spread + EPSILON)
     standard = (pooled - centre) * inverse
     cellbuf = r["cellbuf"]
-    cellbuf[col] = standard.astype(BF16).astype(F32)
+    cellbuf[col] = standard.astype(BF16)
 
     def cell(step):
         return remote(
@@ -196,7 +224,7 @@
 
     for step in range(1, cols_n):
         cell(step).wait()
-    key_cells = cellbuf[...].reshape(cells_n, channels).astype(BF16)
+    key_cells = jnp.concatenate([cellbuf[at].astype(F32) for at in range(cols_n)], axis=0).astype(BF16)
     r["key_all"][row] = key_cells
     r["keys"][...] = contract(key_cells, r["w_key"][...], 1, 0).astype(BF16)
     r["values"][...] = contract(key_cells, r["w_value"][...], 1, 0).astype(BF16)
@@ -442,7 +470,8 @@
         tap_second(step).start()
 
     start_third(1)
-    take_halo(2)
+    wait_edges(2, (True, False))
+    take_cols(2)
 
     @pl.loop(0, channels // LANES)
     def _(part):
@@ -512,10 +541,11 @@
         pad2=((height + 2, width + 2 * EDGE, channels), F32),
         edges_out1=((2, height, channels), F32), edges_in1=((2, height, channels), F32),
         edges_out2=((2, height, channels), F32), edges_in2=((2, height, channels), F32),
+        rows_in1=((2, width, channels), BF16), corners_in1=((4, 2 * EDGE, channels), BF16),
         hidden=((tokens, channels), BF16), query=((tokens, channels), BF16), dout=((tokens, channels), BF16),
         attended=((tokens, channels), BF16), grad_query=((tokens, channels), BF16),
         pooled=((own, channels), F32), over=((height // POOL, width, channels), F32),
-        cellbuf=((cols_n, own, channels), F32),
+        cellbuf=((cols_n, own, channels), BF16),
         keys=((cells_n, channels), BF16), values=((cells_n, channels), BF16),
         blocks=((cols_n, 2 * own, channels), BF16), blocks_in=((cols_n - 1, 2 * own, channels), BF16),
         tot_all=((cols_n, 2 * own, channels), BF16),

time: 78.7 us -> 72.7 us (0.924)
  Pallas kernels: 72.8 us -> 66.8 us
    pallas_call x1, Pallas kernels: 72.8 us -> 66.8 us  [on_device(): pl.pallas_call(partial(block_kernel, rows_n, cols_n, names), out_shape=[j...]
where the time goes in v4:
time: 72.7 us; the launch traced here: 72.5 us
  Pallas kernels  66.8 us (92%)
  matrix products  2.76 us (4%)
  local copies, waits for them, and re-layouts  2.27 us (3%)
    pallas_call x1, Pallas kernels, on_device(): pl.pallas_call(partial(block_kernel, rows_n, cols_n, names), out_shape=[j...  66.8 us
    dot_general x1, matrix products, contract(): lax.dot_general(left, right, (((at_left,), (at_right,)), ((), ())), prefe...  2.76 us

profile of v4, /device:TPU:0, one launch (start us, length us, event | category | flops | bytes accessed | tf_op | source)
XLA Modules:
  0.0 72.5 jit_solution(5897474270387802201)
XLA Ops:
  0.6 66.8 %shard_map.94 = (bf16[16,32,768]{2,1,0:T(8,128)(2,1)}, bf16[4,192,384]{2,1,0:T(8,128)(2,1)}, bf16[4,64,768]{2,1,0:T(8,128)(2,1)}, bf16[4,64,768]{2,1,0:T(8,128)(2,1)}, f32[16,768]{1,0:T(8,128)}) custom-call(bf16[16,32,768]{2,1,0:T(8,128)(2,1)} %refs_0_.1, bf16[512,768]{1,0:T(8,128)(2,1)} %bitcast.7, f32[9,768]{1,0:T(8,128)} %refs_2_.1, ...), custom_call_target="tpu_custom_call" | custom-call | tf_op jit(solution)/shard_map/pallas_call | solution.py:573
  67.5 0.0 copy-start
  67.5 2.8 %convolution_select_fusion = f32[768,384]{1,0:T(8,128)} fusion(bf16[256,768]{1,0:T(8,128)(2,1)} %bitcast.9, bf16[768,384]{1,0:T(8,128)(2,1)} %bitcast.8, pred[]{:T(512)S(6)} %and.5, bf16[256,768]{1,0:T(8,128)(2,1)} %bitcast.10, s32[]{:T(128)S(6)} %select_n.15), kind=kOutput, calls=%fused_computation | convolution fusion | flops 151584768 | bytes 2359301 | tf_op jit(solution)/shard_map/dot_general | solution.py:24
  70.2 1.4 %constant_dynamic-slice_fusion = f32[9,96]{1,0:T(8,128)} fusion(f32[9,768]{1,0:T(8,128)} %bitcast.11, s32[]{:T(128)S(6)} %select_n.17), kind=kLoop, calls=%fused_computation.2 | loop fusion | bytes 6916 | tf_op jit(solution)/shard_map/dynamic_slice | solution.py:592
  71.6 0.0 copy-done
  71.6 0.9 %copy.11 = bf16[16,32,768]{2,1,0:T(8,128)(2,1)} copy(bf16[16,32,768]{2,1,0:T(8,128)(2,1)S(1)} %copy-done) | data formatting | bytes 1572864
Async XLA Ops:
  67.5 4.2 %copy-start = (bf16[16,32,768]{2,1,0:T(8,128)(2,1)S(1)}, bf16[16,32,768]{2,1,0:T(8,128)(2,1)}, u32[]{:S(2)}) copy-start(bf16[16,32,768]{2,1,0:T(8,128)(2,1)} %get-tuple-element.16) | copy-start | bytes 2359300

commit v5 on v4

--- a/solution.py
+++ b/solution.py
@@ -469,19 +469,23 @@
     for step in range(1, cols_n):
         tap_second(step).start()
 
+    def unmix(wanted):
+        @pl.loop(0, channels // LANES)
+        def _(part):
+            lanes = pl.ds(pl.multiple_of(part * LANES, LANES), LANES)
+            weight = [jnp.broadcast_to(taps[i : i + 1, lanes], (width, LANES)) for i in range(9)]
+            for at in wanted:
+                total = pad2[at + 1, middle, lanes]
+                for i in range(9):
+                    total = total + weight[i] * pad2[at + 2 - i // 3, pl.ds(EDGE + 1 - i % 3, width), lanes]
+                r["grad_image"][at, :, lanes] = total.astype(BF16)
+
+    wait_edges(2, (True,))
+    take_cols(2)
+    unmix(range(1, height - 1))
     start_third(1)
-    wait_edges(2, (True, False))
-    take_cols(2)
-
-    @pl.loop(0, channels // LANES)
-    def _(part):
-        lanes = pl.ds(pl.multiple_of(part * LANES, LANES), LANES)
-        weight = [jnp.broadcast_to(taps[i : i + 1, lanes], (width, LANES)) for i in range(9)]
-        for at in range(height):
-            total = pad2[at + 1, middle, lanes]
-            for i in range(9):
-                total = total + weight[i] * pad2[at + 2 - i // 3, pl.ds(EDGE + 1 - i % 3, width), lanes]
-            r["grad_image"][at, :, lanes] = total.astype(BF16)
+    wait_edges(2, (False,))
+    unmix((0, height - 1))
 
     start_fourth(0)
     start_fourth(1)

time: 72.7 us -> 72.8 us (level)
  no operation moved by 1% of the time
where the time goes in v5:
time: 72.8 us; the launch traced here: 72.6 us
  Pallas kernels  66.9 us (92%)
  matrix products  2.76 us (4%)
  local copies, waits for them, and re-layouts  2.27 us (3%)
    pallas_call x1, Pallas kernels, on_device(): pl.pallas_call(partial(block_kernel, rows_n, cols_n, names), out_shape=[j...  66.9 us
    dot_general x1, matrix products, contract(): lax.dot_general(left, right, (((at_left,), (at_right,)), ((), ())), prefe...  2.76 us

profile of v5, /device:TPU:0, one launch (start us, length us, event | category | flops | bytes accessed | tf_op | source)
XLA Modules:
  0.0 72.6 jit_solution(13180562044403063779)
XLA Ops:
  0.6 66.9 %shard_map.94 = (bf16[16,32,768]{2,1,0:T(8,128)(2,1)}, bf16[4,192,384]{2,1,0:T(8,128)(2,1)}, bf16[4,64,768]{2,1,0:T(8,128)(2,1)}, bf16[4,64,768]{2,1,0:T(8,128)(2,1)}, f32[16,768]{1,0:T(8,128)}) custom-call(bf16[16,32,768]{2,1,0:T(8,128)(2,1)} %refs_0_.1, bf16[512,768]{1,0:T(8,128)(2,1)} %bitcast.7, f32[9,768]{1,0:T(8,128)} %refs_2_.1, ...), custom_call_target="tpu_custom_call" | custom-call | tf_op jit(solution)/shard_map/pallas_call | solution.py:577
  67.5 0.0 copy-start
  67.6 2.8 %convolution_select_fusion = f32[768,384]{1,0:T(8,128)} fusion(bf16[256,768]{1,0:T(8,128)(2,1)} %bitcast.9, bf16[768,384]{1,0:T(8,128)(2,1)} %bitcast.8, pred[]{:T(512)S(6)} %and.5, bf16[256,768]{1,0:T(8,128)(2,1)} %bitcast.10, s32[]{:T(128)S(6)} %select_n.15), kind=kOutput, calls=%fused_computation | convolution fusion | flops 151584768 | bytes 2359301 | tf_op jit(solution)/shard_map/dot_general | solution.py:24
  70.3 1.4 %constant_dynamic-slice_fusion = f32[9,96]{1,0:T(8,128)} fusion(f32[9,768]{1,0:T(8,128)} %bitcast.11, s32[]{:T(128)S(6)} %select_n.17), kind=kLoop, calls=%fused_computation.2 | loop fusion | bytes 6916 | tf_op jit(solution)/shard_map/dynamic_slice | solution.py:596
  71.7 0.0 copy-done
  71.7 0.9 %copy.11 = bf16[16,32,768]{2,1,0:T(8,128)(2,1)} copy(bf16[16,32,768]{2,1,0:T(8,128)(2,1)S(1)} %copy-done) | data formatting | bytes 1572864
Async XLA Ops:
  67.5 4.2 %copy-start = (bf16[16,32,768]{2,1,0:T(8,128)(2,1)S(1)}, bf16[16,32,768]{2,1,0:T(8,128)(2,1)}, u32[]{:S(2)}) copy-start(bf16[16,32,768]{2,1,0:T(8,128)(2,1)} %get-tuple-element.16) | copy-start | bytes 2359300
